TPU v7x, 128 devices: a whole 4x4x4 slice. The times are simulated.
128 devices in a mesh: gx: 16 (over y, x), gy: 8 (over z, core).
Axes of the slice: x: 4, y: 4, z: 4, core: 2. Of those that a mesh axis runs over, the one named last changes fastest.
Arguments:
- state_now: float32 [128, 128, 4096], P(('gx', 'gy')), may hold values from -6 to 6
- state_prev: float32 [128, 128, 4096], P(('gx', 'gy')), may hold values from -6 to 6
- pml_flags: int32 [128], P(('gx', 'gy')), may hold values 0 or 1
- interfaces: int32 [256, 6], P(('gx', 'gy')), may hold values from -16 to 16, as said below
Outputs:
- new_state: float32 [128, 128, 4096], P(('gx', 'gy'))
- face_pressure: float32 [128, 6, 4096], P(('gx', 'gy'))
Inputs may be any that keep to these rules, and one draw needn't show every extreme that they name: `interfaces`: column 0 and column 1 are always 0 (each device holds one box); column 1 names the box of the device one step further along gx and g = column 2 steps across gy; g is -1, 0 or 1 and that device exists whenever column 5 is 1. Columns 3 and 4 are offsets from -16 to 16. Column 5 is 0 exactly on the rows of the last index of gx, which join nothing, and 1 elsewhere.
All inputs are finite; a program needn't handle non-finite values. No bound on the sum of `pml_flags` on one device may be relied on, other than what follows from the above.
Results may differ from a plain program's by a relative error of at most 0.0003.
Values sent between devices are 32-bit elements; how exact they have to be, the bound alone decides.
A program may use at most 128 MiB of HBM per device.

v0:
```python
import math

import jax
import jax.numpy as jnp
import numpy as np
from jax import lax
from jax.experimental import pallas as pl
from jax.experimental.pallas import tpu as pltpu
from jax.sharding import PartitionSpec as P

S0 = 128
S1 = 64
S2 = 64
CROSS = S1 * S2
STEPS = 3
TILES = CROSS // 128
PLANE = 32
MESH = pl.DeviceIdType.MESH
F32 = jnp.float32
BF16 = jnp.bfloat16
HIGHEST = lax.Precision.HIGHEST

COURANT2 = 0.16
CENTER3 = 3.0 * (-490.0 / 180.0)
TAPS = (1.5, -0.15, 1.0 / 90.0)
PAIRS = {(0, 0): 0, (0, 1): 1, (0, 2): 2, (1, 1): 3, (1, 2): 4, (2, 2): 5}


def basis(n):
    k = np.arange(n)[:, None]
    i = np.arange(n)[None, :]
    weight = np.where(k == 0, math.sqrt(1.0 / n), math.sqrt(2.0 / n))
    return weight * np.cos(math.pi * k * (i + 0.5) / n)


def twice(a):
    n = a.shape[0]
    out = np.zeros((2 * n, 2 * n))
    out[:n, :n] = a
    out[n:, n:] = a
    return out


def halves(a):
    high = a.astype(np.float32).astype(BF16)
    low = (a - high.astype(np.float64)).astype(np.float32).astype(BF16)
    return high, low


def constants():
    c0, c1 = basis(S0), basis(S1)
    k = (math.pi * np.arange(S0) / S0) ** 2
    a = (math.pi * np.arange(S1) / S1) ** 2
    wave = (k[:, None, None] + a[None, :, None] + a[None, None, :]).reshape(S0, CROSS)
    safe = np.where(wave > 0, wave, 1.0)
    gain = np.where(wave > 0, 4.0 * np.sin(0.2 * np.sqrt(wave)) ** 2 / safe, COURANT2)
    face = c0[:, :3]
    sign = (-1.0) ** np.arange(S0)
    planes = []
    for s in (np.ones(S0), sign):
        for d, e in PAIRS:
            planes.append(((face[:, d] * face[:, e] * s) @ gain).reshape(PLANE, 128))
    order = np.concatenate([np.arange(0, S1, 2), np.arange(1, S1, 2)])
    c1p = c1[order][:, order]
    misc = np.concatenate(
        [np.repeat(face[:, d : d + 1], 128, axis=1) for d in range(3)]
        + planes
        + [twice(c1), twice(c1.T), twice(c1p), twice(c1p.T)],
        axis=0,
    )

    def band(n):
        out = np.zeros((n, n))
        for distance, tap in enumerate(TAPS, 1):
            out += tap * (np.eye(n, k=distance) + np.eye(n, k=-distance))
        return out

    along_hi, along_lo = halves(band(S0))
    inner_hi, inner_lo = halves(twice(twice(band(S2))))
    stencil = np.concatenate(
        [np.concatenate([along_hi, along_lo], axis=1), inner_hi, inner_lo], axis=0
    )
    return gain.astype(np.float32), misc.astype(np.float32), stencil


ROW_FACE, ROW_P, ROW_C = 0, 384, 768


def rate_of(row):
    return 0.5 * ((row + 0.5) / S0) ** 2


FACE_COEF = [COURANT2 / (1.0 + rate_of(i)) for i in (0, 1, 2, 127, 126, 125)]


def split(x):
    high = x.astype(BF16)
    return high, (x - high.astype(F32)).astype(BF16)


def dot(a, b):
    return jnp.dot(a, b, preferred_element_type=F32)


def top_dot(a, b):
    return jnp.dot(a, b, preferred_element_type=F32, precision=HIGHEST)


def couple(p):
    w1, w2, w3 = TAPS
    return [w1 * p[0] + w2 * p[1] + w3 * p[2], w2 * p[0] + w3 * p[1], w3 * p[0]]


def kernel(
    flags, faces, now_hbm, prev_hbm, gain_hbm, misc_hbm, stencil_hbm,
    out, layers_out,
    state, gain, slow, misc, stencil, halved, rolled, rows,
    acc, picked, spread, free, left, right, flag_out, flag_in, layers, sums, low_in, force_in, outp,
    load_sem, send_sem, recv_sem,
):
    gx, gy = lax.axis_index("gx"), lax.axis_index("gy")
    nx, ny = lax.axis_size("gx"), lax.axis_size("gy")
    inner = pl.ds(128, CROSS)

    loads = [
        pltpu.make_async_copy(misc_hbm, misc, load_sem.at[0]),
        pltpu.make_async_copy(now_hbm.at[0], state.at[0, :, inner], load_sem.at[1]),
        pltpu.make_async_copy(stencil_hbm, stencil, load_sem.at[2]),
        pltpu.make_async_copy(prev_hbm.at[0], state.at[1, :, inner], load_sem.at[3]),
        pltpu.make_async_copy(gain_hbm, gain, load_sem.at[4]),
    ]
    for load in loads:
        load.start()

    low_in[...] = jnp.zeros_like(low_in)
    force_in[...] = jnp.zeros_like(force_in)
    flag_in[...] = jnp.zeros_like(flag_in)
    flag_out[...] = jnp.full(flag_out.shape, flags[0], jnp.int32).astype(F32)

    back_ok, ahead_ok = gx > 0, gx < nx - 1
    side_ok = {-1: gy > 0, 0: gy >= 0, 1: gy < ny - 1}
    barrier = pltpu.get_barrier_semaphore()
    for ok, to_x in ((back_ok, gx - 1), (ahead_ok, gx + 1)):
        for side in (-1, 0, 1):

            @pl.when(jnp.logical_and(ok, side_ok[side]))
            def _():
                pl.semaphore_signal(barrier, inc=1, device_id=(to_x, gy + side), device_id_type=MESH)

    sides = 1 + (gy > 0).astype(jnp.int32) + (gy < ny - 1).astype(jnp.int32)
    ends = (gx > 0).astype(jnp.int32) + (gx < nx - 1).astype(jnp.int32)
    pl.semaphore_wait(barrier, sides * ends)

    def back(source, target, sem, g):
        return pltpu.make_async_remote_copy(
            src_ref=source, dst_ref=target, send_sem=send_sem.at[sem], recv_sem=recv_sem.at[sem],
            device_id=(gx - 1, gy - g), device_id_type=MESH,
        )

    def ahead(source, target, sem, g):
        return pltpu.make_async_remote_copy(
            src_ref=source, dst_ref=target, send_sem=send_sem.at[sem], recv_sem=recv_sem.at[sem],
            device_id=(gx + 1, gy + g), device_id_type=MESH,
        )

    def flag_copy(g):
        return back(flag_out, flag_in.at[g + 1], g + 1, g)

    def low_copy(n, g):
        return back(layers.at[n, pl.ds(0, 96)], low_in.at[n, g + 1], 3 + 3 * n + g + 1, g)

    def force_copy(n, g):
        return ahead(sums.at[n, g + 1], force_in.at[n, g + 1], 12 + 3 * n + g + 1, g)

    def send_back(copy):
        for g in (-1, 0, 1):

            @pl.when(jnp.logical_and(back_ok, side_ok[-g]))
            def _():
                copy(g).start()

    def got_back(copy):
        for g in (-1, 0, 1):

            @pl.when(jnp.logical_and(ahead_ok, side_ok[g]))
            def _():
                copy(g).wait_recv()

    def send_ahead(copy):
        for g in (-1, 0, 1):

            @pl.when(jnp.logical_and(ahead_ok, side_ok[g]))
            def _():
                copy(g).start()

    def got_ahead(copy):
        for g in (-1, 0, 1):

            @pl.when(jnp.logical_and(back_ok, side_ok[-g]))
            def _():
                copy(g).wait_recv()

    send_back(flag_copy)

    def is_pml(shape):
        return jnp.full(shape, flags[0], jnp.int32) > 0

    lanes = lax.broadcasted_iota(jnp.int32, (PLANE, 128), 1)
    first = lanes < 64

    def fb(d):
        return misc[ROW_FACE + d * 128 : ROW_FACE + (d + 1) * 128, :].reshape(16, 8, 128)

    def note_faces(block, c):
        tiles = block.reshape(16, 8, 128)
        for d in range(3):
            acc[pl.ds(d * 256 + c, 8, stride=PLANE), :] = jnp.sum(fb(d) * tiles, axis=0)
        picked[pl.ds(c, 8, stride=PLANE), :] = block[0:8, :]
        picked[pl.ds(256 + c, 8, stride=PLANE), :] = block[120:128, :]

    def gathered_faces():
        low, high = [], []
        pml = is_pml((PLANE, 128))
        for d in range(3):
            part = [acc[d * 256 + s * 32 : d * 256 + (s + 1) * 32, :] for s in range(8)]
            even = (part[0] + part[2]) + (part[4] + part[6])
            odd = (part[1] + part[3]) + (part[5] + part[7])
            row_low = picked[d * 32 : (d + 1) * 32, :]
            row_high = picked[256 + (7 - d) * 32 : 256 + (8 - d) * 32, :]
            low.append(jnp.where(pml, row_low, even + odd))
            high.append(jnp.where(pml, row_high, even - odd))
        return low + high

    loads[0].wait()
    loads[1].wait()

    def tile(c):
        return pl.ds(pl.multiple_of(c * 128, 128), 128)

    @pl.loop(0, TILES // 2)
    def _(t):
        for h in range(2):
            c = 2 * t + h
            note_faces(state[0, :, tile(c + 1)], c)

    for e, plane in enumerate(gathered_faces()):
        layers[0, e * 32 : (e + 1) * 32, :] = plane
    send_back(lambda g: low_copy(0, g))

    got_back(flag_copy)
    big_row = lax.broadcasted_iota(jnp.int32, (128, 128), 0)
    big_col = lax.broadcasted_iota(jnp.int32, (128, 128), 1)
    same = (big_row >> 6) == (big_col >> 6)
    eye = jnp.where(big_row == big_col, 1.0, 0.0).astype(F32)
    own = is_pml((128, 128))
    ours, ours_t, ours_p, ours_pt = (
        jnp.where(own, eye, misc[ROW_C + i * 128 : ROW_C + (i + 1) * 128, :]) for i in range(4)
    )

    def theirs(r):
        g = jnp.full((8, 128), faces[r, 2], jnp.int32)
        value = jnp.where(g == -1, flag_in[0], jnp.where(g == 0, flag_in[1], flag_in[2]))
        return jnp.broadcast_to(value[0:1, :], (128, 128)) > 0.5

    their = [theirs(r) for r in range(2)]
    q_row, q_col = big_row & 63, big_col & 63
    j_row = 2 * (q_row & 31) + (q_row >> 5)
    j_col = 2 * (q_col & 31) + (q_col >> 5)
    upper = big_row < 64
    step_one = jnp.where(
        upper,
        jnp.full((128, 128), faces[0, 3], jnp.int32),
        jnp.full((128, 128), faces[1, 3], jnp.int32),
    )
    shift_one = jnp.where(jnp.logical_and(same, j_col == j_row - step_one), 1.0, 0.0).astype(F32)
    their_pt = jnp.where(
        jnp.where(upper, their[0].astype(F32), their[1].astype(F32)) > 0.5,
        eye,
        misc[ROW_C + 3 * 128 : ROW_C + 4 * 128, :],
    )
    cross_one = top_dot(ours_p, top_dot(shift_one, their_pt))

    def keep_left(i, matrix):
        hi, lo = split(matrix)
        left[i, :, 0:128] = hi
        left[i, :, 128:256] = hi
        left[i, :, 256:384] = lo

    def keep_right(i, matrix):
        hi, lo = split(matrix)
        right[i, 0:128, :] = hi
        right[i, 128:256, :] = hi
        right[i, 256:384, :] = lo

    keep_left(0, cross_one)
    keep_left(1, cross_one.T)
    for r in range(2):
        step_two = jnp.full((128, 128), faces[r, 4], jnp.int32)
        shift_two = jnp.where(jnp.logical_and(same, q_row == q_col - step_two), 1.0, 0.0).astype(F32)
        their_c = jnp.where(their[r], eye, misc[ROW_C : ROW_C + 128, :])
        cross_two = top_dot(their_c, top_dot(shift_two, ours_t))
        keep_right(r, cross_two)
        keep_right(2 + r, cross_two.T)
    keep_left(2, ours_pt)
    keep_right(4, ours)

    def chosen(r, g):
        hit = jnp.logical_and(
            jnp.full((96, 128), faces[r, 2], jnp.int32) == g,
            jnp.full((96, 128), faces[r, 5], jnp.int32) > 0,
        )
        return hit

    def stacked(x):
        hi, lo = split(x)
        return jnp.concatenate([hi, lo, hi], axis=1)

    def columns(first_rows, second_rows):
        outer = []
        for w in (first_rows, second_rows):
            even, odd = [], []
            for e in range(3):
                p = w[e * 32 : (e + 1) * 32, :]
                swapped = pltpu.roll(p, 64, 1)
                even.append(jnp.where(first, p, swapped))
                odd.append(jnp.where(first, swapped, p))
            outer.append(jnp.concatenate(even, axis=1))
            outer.append(jnp.concatenate(odd, axis=1))
        hi, lo = split(jnp.concatenate(outer, axis=0))
        return jnp.concatenate([hi, lo, hi], axis=0)

    def planes_of(product, s):
        top = product[64 * s : 64 * s + 32, :]
        bottom = product[64 * s + 32 : 64 * s + 64, :]
        return [
            jnp.where(first, top[:, e * 128 : (e + 1) * 128], bottom[:, e * 128 : (e + 1) * 128])
            for e in range(3)
        ]

    def make_sums(n):
        z = couple([layers[n, (3 + d) * 32 : (4 + d) * 32, :] for d in range(3)])
        z3 = stacked(jnp.concatenate(z, axis=0))
        product = dot(left[1], columns(dot(z3, right[2]), dot(z3, right[3])))
        moved = [jnp.concatenate(planes_of(product, r), axis=0) for r in range(2)]
        for g in (-1, 0, 1):
            total = jnp.where(chosen(0, g), moved[0], 0.0) + jnp.where(chosen(1, g), moved[1], 0.0)
            sums[n, g + 1] = total

    def high_force(n):
        parts = []
        for r in range(2):
            pick = jnp.zeros((96, 128), F32)
            for g in (-1, 0, 1):
                pick = jnp.where(chosen(r, g), low_in[n, g + 1], pick)
            parts.append(dot(stacked(pick), right[r]))
        product = dot(left[0], columns(parts[0], parts[1]))
        a, b = planes_of(product, 0), planes_of(product, 1)
        return couple([x + y for x, y in zip(a, b)])

    def response(force):
        pml = is_pml((PLANE, 128))
        low, high = [], []
        for d in range(3):
            near, far = 0.0, 0.0
            for e in range(3):
                i = PAIRS[(min(d, e), max(d, e))]
                p = misc[ROW_P + i * 32 : ROW_P + (i + 1) * 32, :]
                q = misc[ROW_P + 192 + i * 32 : ROW_P + 192 + (i + 1) * 32, :]
                near = near + (p * force[e] + q * force[3 + e])
                far = far + (q * force[e] + p * force[3 + e])
            low.append(jnp.where(pml, FACE_COEF[d] * force[d], near))
            high.append(jnp.where(pml, FACE_COEF[3 + d] * force[3 + d], far))
        return low + high

    make_sums(0)
    send_ahead(lambda g: force_copy(0, g))

    k = big_row.astype(F32)
    rate = 0.5 * ((k + 0.5) * (1.0 / S0)) ** 2
    inverse = 1.0 / (1.0 + rate)
    rows[0] = jnp.where(own, (2.0 + COURANT2 * CENTER3) * inverse, 2.0)
    rows[1] = jnp.where(own, (1.0 - rate) * inverse, 1.0)
    rows[2] = jnp.where(own, COURANT2 * inverse, 0.0)
    edge = jnp.zeros((S0, 128), F32)
    for b in range(2):
        state[b, :, 0:128] = edge
        state[b, :, 128 + CROSS : 256 + CROSS] = edge
    for c in (0, 1, TILES + 2, TILES + 3):
        rolled[:, c * 128 : (c + 1) * 128] = edge
    spread[...] = jnp.zeros_like(spread)
    loads[4].wait()

    @pl.loop(0, TILES)
    def _(c):
        col = c * 128 + big_col
        mode_a = (col >> 6).astype(F32) * (math.pi / S1)
        mode_b = (col & 63).astype(F32) * (math.pi / S2)
        mode_k = k * (math.pi / S0)
        masked = jnp.where(own, 0.0, gain[:, tile(c)])
        gain[:, tile(c)] = masked
        slow[:, tile(c)] = masked * (mode_k * mode_k + mode_a * mode_a + mode_b * mode_b)

    loads[2].wait()
    loads[3].wait()

    alternate = (lax.broadcasted_iota(jnp.int32, (8, 128), 0) & 1) == 0

    def forced(block, c):
        total = None
        for d in range(3):
            plus = jnp.broadcast_to(outp[pl.ds(d * 32 + c, 1), :], (8, 128))
            minus = jnp.broadcast_to(outp[pl.ds(96 + d * 32 + c, 1), :], (8, 128))
            term = fb(d) * jnp.where(alternate, plus, minus)[None]
            total = term if total is None else total + term
        block = block + gain[:, tile(c)] * total.reshape(128, 128)
        top = block[0:8, :] + spread[pl.ds(c, 8, stride=PLANE), :]
        bottom = block[120:128, :] + spread[pl.ds(256 + c, 8, stride=PLANE), :]
        return jnp.concatenate([top, block[8:120, :], bottom], axis=0)

    def keep_force(force):
        pml = is_pml((PLANE, 128))
        for d in range(3):
            outp[d * 32 : (d + 1) * 32, :] = force[d] + force[3 + d]
            outp[96 + d * 32 : 96 + (d + 1) * 32, :] = force[d] - force[3 + d]
            spread[d * 32 : (d + 1) * 32, :] = jnp.where(pml, FACE_COEF[d] * force[d], 0.0)
            at = 256 + (7 - d) * 32
            spread[at : at + 32, :] = jnp.where(pml, FACE_COEF[3 + d] * force[3 + d], 0.0)

    def finish_state(b, n):
        @pl.loop(0, TILES // 2)
        def _(t):
            for h in range(2):
                c = 2 * t + h
                block = state[b, :, tile(c + 1)]
                if n > 0:
                    block = forced(block, c)
                    state[b, :, tile(c + 1)] = block
                hi, lo = split(block)
                halved[0:128, tile(c)] = hi
                halved[128:256, tile(c)] = lo
                rolled[:, tile(c + 2)] = pltpu.roll(block, 64, 1)

    w1, w2, w3 = TAPS
    big_first = big_col < 64

    def advance(b, p):
        @pl.loop(0, TILES // 2)
        def _(t):
            wide = pl.ds(pl.multiple_of(t * 256, 256), 256)
            pair = halved[:, wide]
            hi, lo = pair[0:128, :], pair[128:256, :]
            along = stencil[0:128, :]
            twice_hi = jnp.concatenate([along[:, 0:128], along[:, 0:128]], axis=1)
            taps = dot(twice_hi, pair) + dot(along[:, 128:256], hi)
            taps += dot(hi, stencil[128:384, :]) + dot(lo, stencil[128:384, :])
            taps += dot(hi, stencil[384:640, :])
            ring = [rolled[:, tile(2 * t + i)] for i in range(6)]
            quads = [w1 * (ring[i + 2] + ring[i + 1]) + w3 * (ring[i + 3] + ring[i]) for i in range(3)]
            for h in range(2):
                c = 2 * t + h
                block = state[b, :, tile(c + 1)]
                sides_ = state[b, :, tile(c)] + state[b, :, tile(c + 2)]
                stencil_sum = taps[:, h * 128 : (h + 1) * 128] + w2 * sides_
                stencil_sum += jnp.where(big_first, quads[h], quads[h + 1])
                following = (rows[0] - slow[:, tile(c)]) * block - rows[1] * state[p, :, tile(c + 1)]
                following += rows[2] * stencil_sum
                state[p, :, tile(c + 1)] = following
                note_faces(following, c)

        for e, plane in enumerate(gathered_faces()):
            free[e * 32 : (e + 1) * 32, :] = plane

    for n in range(STEPS):
        b, p = n % 2, 1 - n % 2
        if n > 0:
            send_back(lambda g: low_copy(n, g))
            make_sums(n)
            send_ahead(lambda g: force_copy(n, g))
        finish_state(b, n)
        advance(b, p)
        got_back(lambda g: low_copy(n, g))
        high = high_force(n)
        got_ahead(lambda g: force_copy(n, g))
        low = [
            force_in[n, 0, e * 32 : (e + 1) * 32, :]
            + force_in[n, 1, e * 32 : (e + 1) * 32, :]
            + force_in[n, 2, e * 32 : (e + 1) * 32, :]
            for e in range(3)
        ]
        force = low + high
        for e, plane in enumerate(response(force)):
            at = slice(e * 32, (e + 1) * 32)
            layers[n + 1, at, :] = free[at, :] + plane
        keep_force(force)

    last = STEPS % 2

    @pl.loop(0, TILES // 2)
    def _(t):
        for h in range(2):
            c = 2 * t + h
            out[0, :, tile(c)] = forced(state[last, :, tile(c + 1)], c)

    final = layers[STEPS]
    turned = dot(stacked(final), right[4])
    product = dot(left[2], columns(turned[0:96, :], turned[96:192, :]))
    for s in range(2):
        for e, plane in enumerate(planes_of(product, s)):
            at = (3 * s + e) * 32
            outp[at : at + 32, :] = plane

    @pl.loop(0, TILES)
    def _(c):
        layers_out[0, :, tile(c)] = outp[pl.ds(c, 8, stride=PLANE), :][0:6, :]

    for g in (-1, 0, 1):

        @pl.when(jnp.logical_and(back_ok, side_ok[-g]))
        def _():
            flag_copy(g).wait_send()
            for n in range(STEPS):
                low_copy(n, g).wait_send()

        @pl.when(jnp.logical_and(ahead_ok, side_ok[g]))
        def _():
            for n in range(STEPS):
                force_copy(n, g).wait_send()


def local(state_now, state_prev, pml_flags, interfaces):
    gain, misc, stencil = constants()
    smem = pl.BlockSpec(memory_space=pltpu.SMEM)
    hbm = pl.BlockSpec(memory_space=pl.ANY)
    vmem = pl.BlockSpec(memory_space=pltpu.VMEM)
    return pl.pallas_call(
        kernel,
        out_shape=(
            jax.ShapeDtypeStruct((1, S0, CROSS), F32),
            jax.ShapeDtypeStruct((1, 6, CROSS), F32),
        ),
        in_specs=[smem, smem, hbm, hbm, hbm, hbm, hbm],
        out_specs=(vmem, vmem),
        scratch_shapes=[
            pltpu.VMEM((2, S0, CROSS + 256), F32),
            pltpu.VMEM((S0, CROSS), F32),
            pltpu.VMEM((S0, CROSS), F32),
            pltpu.VMEM(misc.shape, F32),
            pltpu.VMEM(stencil.shape, BF16),
            pltpu.VMEM((256, CROSS), BF16),
            pltpu.VMEM((S0, CROSS + 512), F32),
            pltpu.VMEM((3, 128, 128), F32),
            pltpu.VMEM((768, 128), F32),
            pltpu.VMEM((512, 128), F32),
            pltpu.VMEM((512, 128), F32),
            pltpu.VMEM((192, 128), F32),
            pltpu.VMEM((3, 128, 384), BF16),
            pltpu.VMEM((5, 384, 128), BF16),
            pltpu.VMEM((8, 128), F32),
            pltpu.VMEM((3, 8, 128), F32),
            pltpu.VMEM((STEPS + 1, 192, 128), F32),
            pltpu.VMEM((STEPS, 3, 96, 128), F32),
            pltpu.VMEM((STEPS, 3, 96, 128), F32),
            pltpu.VMEM((STEPS, 3, 96, 128), F32),
            pltpu.VMEM((256, 128), F32),
            pltpu.SemaphoreType.DMA((5,)),
            pltpu.SemaphoreType.DMA((21,)),
            pltpu.SemaphoreType.DMA((21,)),
        ],
        compiler_params=pltpu.CompilerParams(
            collective_id=0, has_side_effects=True, vmem_limit_bytes=56 * 1024 * 1024
        ),
    )(pml_flags, interfaces, state_now, state_prev, jnp.asarray(gain), jnp.asarray(misc), jnp.asarray(stencil))


def solution(mesh):
    one, two, three = P(("gx", "gy")), P(("gx", "gy"), None), P(("gx", "gy"), None, None)
    return jax.shard_map(
        local,
        mesh=mesh,
        in_specs=(three, three, one, two),
        out_specs=(three, three),
        check_vma=False,
    )
```

profile of v0, /device:TPU:55, one launch (start us, length us, event | category | flops | bytes accessed | tf_op | source)
XLA Modules:
  0.0 46.4 jit_solution(377074202271636356)
XLA Ops:
  1.3 40.4 %shard_map.86 = (f32[1,128,4096]{2,1,0:T(8,128)}, f32[1,6,4096]{2,1,0:T(8,128)}) custom-call(s32[1]{0:T(128)S(6)} %copy.11.flags, s32[2,6]{1,0:T(2,128)} %faces.1, f32[1,128,4096]{2,1,0:T(8,128)} %now_hbm.1, f32[1,128,4096]{2,1,0:T(8,128)} %prev_hbm.1, f32[128,4096]{1,0:T(8,128)} %constant.6.clone.gain_hbm, f32[1280,128]{1,0:T(8,128)} %constant.7.clone.misc_hbm, ...), custom_call_target="tpu_custom_call" | custom-call | tf_op jit(solution)/shard_map/pallas_call | solution.py:535
  41.6 1.6 %copy.9 = f32[1,6,4096]{2,0,1:T(1,128)} copy(f32[1,6,4096]{2,1,0:T(8,128)} %get-tuple-element.3) | data formatting | bytes 196608 | tf_op jit(solution)/shard_map/pallas_call | solution.py:535
  43.3 3.1 %copy.12 = f32[1,128,4096]{2,1,0:T(8,128)} copy(f32[1,128,4096]{2,1,0:T(8,128)} %get-tuple-element.6) | data formatting | bytes 4194304
where the time goes:
time: 46.7 us; the launch traced here: 46.4 us
  Pallas kernels  40.4 us (87%)
  local copies, waits for them, and re-layouts  4.76 us (10%)
  between operations  1.28 us (3%)
    pallas_call x1, Pallas kernels, local(): pl.pallas_call(kernel, out_shape=(jax.ShapeDtypeStruct((1, S0, CROSS), F3...  40.4 us
    unnamed x1, local copies, waits for them, and re-layouts  3.11 us
    pallas_call x1, local copies, waits for them, and re-layouts, local(): pl.pallas_call(kernel, out_shape=(jax.ShapeDtypeStruct((1, S0, CROSS), F3...  1.65 us

commit v1 on v0

v1 whole, which is shorter than its diff:
```python
import math

import jax
import jax.numpy as jnp
import numpy as np
from jax import lax
from jax.experimental import pallas as pl
from jax.experimental.pallas import tpu as pltpu
from jax.sharding import PartitionSpec as P

S0 = 128
S1 = 64
S2 = 64
CROSS = S1 * S2
STEPS = 3
TILES = CROSS // 128
PLANE = 32
MESH = pl.DeviceIdType.MESH
F32 = jnp.float32
BF16 = jnp.bfloat16

COURANT2 = 0.16
CENTER3 = 3.0 * (-490.0 / 180.0)
TAPS = (1.5, -0.15, 1.0 / 90.0)
TAPS_90 = (135.0, -13.5, 1.0)
PAIRS = {(0, 0): 0, (0, 1): 1, (0, 2): 2, (1, 1): 3, (1, 2): 4, (2, 2): 5}


def basis(n):
    k = np.arange(n)[:, None]
    i = np.arange(n)[None, :]
    weight = np.where(k == 0, math.sqrt(1.0 / n), math.sqrt(2.0 / n))
    return weight * np.cos(math.pi * k * (i + 0.5) / n)


def twice(a):
    n = a.shape[0]
    out = np.zeros((2 * n, 2 * n))
    out[:n, :n] = a
    out[n:, n:] = a
    return out


def constants():
    c0, c1 = basis(S0), basis(S1)
    k = (math.pi * np.arange(S0) / S0) ** 2
    a = (math.pi * np.arange(S1) / S1) ** 2
    wave = (k[:, None, None] + a[None, :, None] + a[None, None, :]).reshape(S0, CROSS)
    safe = np.where(wave > 0, wave, 1.0)
    gain = np.where(wave > 0, 4.0 * np.sin(0.2 * np.sqrt(wave)) ** 2 / safe, COURANT2)
    face = c0[:, :3]
    sign = (-1.0) ** np.arange(S0)
    planes = []
    for s in (np.ones(S0), sign):
        for d, e in PAIRS:
            planes.append(((face[:, d] * face[:, e] * s) @ gain).reshape(PLANE, 128))
    order = np.concatenate([np.arange(0, S1, 2), np.arange(1, S1, 2)])
    c1p = c1[order][:, order]
    misc = np.concatenate(
        [np.repeat(face[:, d : d + 1], 128, axis=1) for d in range(3)]
        + planes
        + [twice(c1), twice(c1.T), twice(c1p), twice(c1p.T)],
        axis=0,
    )

    def band(n):
        out = np.zeros((n, n))
        for distance, tap in enumerate(TAPS_90, 1):
            out += tap * (np.eye(n, k=distance) + np.eye(n, k=-distance))
        return out

    along = band(S0)
    stencil = np.concatenate([np.concatenate([along, along], axis=1), twice(twice(band(S2)))], axis=0)
    return gain.astype(np.float32), misc.astype(np.float32), stencil.astype(BF16)


ROW_FACE, ROW_P, ROW_C = 0, 384, 768


def rate_of(row):
    return 0.5 * ((row + 0.5) / S0) ** 2


FACE_COEF = [COURANT2 / (1.0 + rate_of(i)) for i in (0, 1, 2, 127, 126, 125)]


def split(x):
    high = x.astype(BF16)
    return high, (x - high.astype(F32)).astype(BF16)


def dot(a, b):
    return jnp.dot(a, b, preferred_element_type=F32)


def couple(p):
    w1, w2, w3 = TAPS
    return [w1 * p[0] + w2 * p[1] + w3 * p[2], w2 * p[0] + w3 * p[1], w3 * p[0]]


def stacked(x):
    hi, lo = split(x)
    return jnp.concatenate([hi, lo, hi], axis=1)


def first_half():
    return lax.broadcasted_iota(jnp.int32, (PLANE, 128), 1) < 64


def columns(*sets):
    first = first_half()
    outer = []
    for w in sets:
        even, odd = [], []
        for e in range(3):
            p = w[e * 32 : (e + 1) * 32, :]
            swapped = pltpu.roll(p, 64, 1)
            even.append(jnp.where(first, p, swapped))
            odd.append(jnp.where(first, swapped, p))
        outer.append(jnp.concatenate(even, axis=1))
        outer.append(jnp.concatenate(odd, axis=1))
    hi, lo = split(jnp.concatenate(outer, axis=0))
    return jnp.concatenate([hi, lo, hi], axis=0)


def planes_of(product, s):
    first = first_half()
    top = product[64 * s : 64 * s + 32, :]
    bottom = product[64 * s + 32 : 64 * s + 64, :]
    return [
        jnp.where(first, top[:, e * 128 : (e + 1) * 128], bottom[:, e * 128 : (e + 1) * 128])
        for e in range(3)
    ]


def left_form(matrix):
    hi, lo = split(matrix)
    return jnp.concatenate([hi, hi, lo], axis=1)


def right_form(matrix):
    hi, lo = split(matrix)
    return jnp.concatenate([hi, hi, lo], axis=0)


def exchange(
    flags, faces_hbm, now_hbm, prev_hbm, gain_hbm, misc_hbm, stencil_hbm,
    free_out, pack_out,
    state, gain, slow, misc, stencil, halved, rolled, rows,
    acc, picked, free, left, right, flag_out, flag_in, layers, sums, low_in, force_in, pack,
    faces, load_sem, send_sem, recv_sem, out_sem,
):
    gx, gy = lax.axis_index("gx"), lax.axis_index("gy")
    nx, ny = lax.axis_size("gx"), lax.axis_size("gy")

    back_ok, ahead_ok = gx > 0, gx < nx - 1
    side_ok = {-1: gy > 0, 0: gy >= 0, 1: gy < ny - 1}
    barrier = pltpu.get_barrier_semaphore()
    for ok, to_x in ((back_ok, gx - 1), (ahead_ok, gx + 1)):
        for side in (-1, 0, 1):

            @pl.when(jnp.logical_and(ok, side_ok[side]))
            def _():
                pl.semaphore_signal(barrier, inc=1, device_id=(to_x, gy + side), device_id_type=MESH)

    head = pltpu.make_async_copy(misc_hbm, misc, load_sem.at[0])
    head.start()
    listed = pltpu.make_async_copy(faces_hbm, faces, load_sem.at[8])
    listed.start()
    chunk = CROSS // 4
    nows = [
        pltpu.make_async_copy(
            now_hbm.at[0, :, pl.ds(i * chunk, chunk)],
            state.at[0, :, pl.ds(128 + i * chunk, chunk)],
            load_sem.at[4 + i],
        )
        for i in range(4)
    ]
    for load in nows:
        load.start()
    rest = [
        pltpu.make_async_copy(gain_hbm, gain, load_sem.at[1]),
        pltpu.make_async_copy(prev_hbm.at[0], state.at[1, :, pl.ds(128, CROSS)], load_sem.at[2]),
        pltpu.make_async_copy(stencil_hbm, stencil, load_sem.at[3]),
    ]
    for load in rest:
        load.start()
    flag_out[...] = jnp.full(flag_out.shape, flags[0], jnp.int32).astype(F32)

    core = lax.rem(gy, 2)
    away = 2 * core - 1
    away_ok = jnp.where(core == 0, gy > 0, gy < ny - 1)
    order = ((away, away_ok), (-away, gy >= 0), (0, gy >= 0))

    def back(source, target, sem, g):
        return pltpu.make_async_remote_copy(
            src_ref=source, dst_ref=target, send_sem=send_sem.at[sem], recv_sem=recv_sem.at[sem],
            device_id=(gx - 1, gy - g), device_id_type=MESH,
        )

    def ahead(source, target, sem, g):
        return pltpu.make_async_remote_copy(
            src_ref=source, dst_ref=target, send_sem=send_sem.at[sem], recv_sem=recv_sem.at[sem],
            device_id=(gx + 1, gy + g), device_id_type=MESH,
        )

    def flag_copy(g):
        return back(flag_out, flag_in.at[g + 1], g + 1, g)

    def low_copy(n, g):
        return back(layers.at[n, pl.ds(0, 96)], low_in.at[n, g + 1], 3 + 3 * n + g + 1, g)

    def force_copy(n, g):
        return ahead(sums.at[n, g + 1], force_in.at[n, g + 1], 12 + 3 * n + g + 1, g)

    def send_back(copy):
        for side, ok in order:

            @pl.when(jnp.logical_and(back_ok, ok))
            def _():
                copy(-side).start()

    def got_back(copy):
        for g in (-1, 0, 1):

            @pl.when(jnp.logical_and(ahead_ok, side_ok[g]))
            def _():
                copy(g).wait_recv()

    def send_ahead(copy):
        for side, ok in order:

            @pl.when(jnp.logical_and(ahead_ok, ok))
            def _():
                copy(side).start()

    def got_ahead(copy):
        for g in (-1, 0, 1):

            @pl.when(jnp.logical_and(back_ok, side_ok[-g]))
            def _():
                copy(g).wait_recv()

    def is_pml(shape):
        return jnp.full(shape, flags[0], jnp.int32) > 0

    listed.wait()
    head.wait()
    big_row = lax.broadcasted_iota(jnp.int32, (128, 128), 0)
    big_col = lax.broadcasted_iota(jnp.int32, (128, 128), 1)
    same = (big_row >> 6) == (big_col >> 6)
    eye = jnp.where(big_row == big_col, 1.0, 0.0).astype(F32)
    own = is_pml((128, 128))
    basis_c, basis_ct, basis_p, basis_pt = (
        misc[ROW_C + i * 128 : ROW_C + (i + 1) * 128, :] for i in range(4)
    )
    ours, ours_t, ours_p, ours_pt = (
        jnp.where(own, eye, m) for m in (basis_c, basis_ct, basis_p, basis_pt)
    )
    q_row, q_col = big_row & 63, big_col & 63
    j_row = 2 * (q_row & 31) + (q_row >> 5)
    j_col = 2 * (q_col & 31) + (q_col >> 5)
    upper = big_row < 64
    step_one = jnp.where(
        upper,
        jnp.full((128, 128), faces[0, 3], jnp.int32),
        jnp.full((128, 128), faces[1, 3], jnp.int32),
    )

    def one_hot(where):
        return jnp.where(where, 1.0, 0.0).astype(BF16)

    def by_exact(a, b):
        hi, lo = split(a)
        return dot(jnp.concatenate([hi, lo], axis=1), jnp.concatenate([b, b], axis=0))

    def exact_by(a, b):
        hi, lo = split(b)
        return dot(jnp.concatenate([a, a], axis=1), jnp.concatenate([hi, lo], axis=0))

    one_pml = by_exact(ours_p, one_hot(jnp.logical_and(same, j_col == j_row - step_one)))
    one_air = dot(stacked(one_pml), right_form(basis_pt))
    two_pml, two_air = [], []
    for r in range(2):
        step_two = jnp.full((128, 128), faces[r, 4], jnp.int32)
        two_pml.append(exact_by(one_hot(jnp.logical_and(same, q_row == q_col - step_two)), ours_t))
        two_air.append(dot(stacked(basis_c), right_form(two_pml[r])))

    left[1] = left_form(one_pml.T)
    right[2] = right_form(two_pml[0].T)
    right[3] = right_form(two_pml[1].T)

    sides = 1 + (gy > 0).astype(jnp.int32) + (gy < ny - 1).astype(jnp.int32)
    ends = (gx > 0).astype(jnp.int32) + (gx < nx - 1).astype(jnp.int32)
    pl.semaphore_wait(barrier, sides * ends)
    send_back(flag_copy)

    def note_faces(partial, top, bottom, c):
        for d in range(3):
            acc[pl.ds(d * 256 + c, 8, stride=PLANE), :] = partial[d]
        picked[pl.ds(c, 8, stride=PLANE), :] = top
        picked[pl.ds(256 + c, 8, stride=PLANE), :] = bottom

    def face_part(partial, chunk_rows, r):
        tiles = chunk_rows.reshape(4, 8, 128)
        out = []
        for d in range(3):
            at = ROW_FACE + d * 128 + 32 * r
            weights = misc[at : at + 32, :].reshape(4, 8, 128)
            term = jnp.sum(weights * tiles, axis=0)
            out.append(term if partial is None else partial[d] + term)
        return out

    def gathered_faces():
        low, high = [], []
        pml = is_pml((PLANE, 128))
        for d in range(3):
            part = [acc[d * 256 + s * 32 : d * 256 + (s + 1) * 32, :] for s in range(8)]
            even = (part[0] + part[2]) + (part[4] + part[6])
            odd = (part[1] + part[3]) + (part[5] + part[7])
            row_low = picked[d * 32 : (d + 1) * 32, :]
            row_high = picked[256 + (7 - d) * 32 : 256 + (8 - d) * 32, :]
            low.append(jnp.where(pml, row_low, even + odd))
            high.append(jnp.where(pml, row_high, even - odd))
        return low + high

    for i in range(4):
        nows[i].wait()

        @pl.loop(0, TILES // 8)
        def _(t):
            window = state.at[0, :, pl.ds(pl.multiple_of(128 + i * chunk + t * 256, 128), 256)]
            for h in range(2):
                at = slice(h * 128, (h + 1) * 128)
                partial = None
                for r in range(4):
                    partial = face_part(partial, window[32 * r : 32 * r + 32, at], r)
                note_faces(partial, window[0:8, at], window[120:128, at], 8 * i + 2 * t + h)

    for e, plane in enumerate(gathered_faces()):
        layers[0, e * 32 : (e + 1) * 32, :] = plane
    send_back(lambda g: low_copy(0, g))

    def chosen(r, g):
        return jnp.logical_and(
            jnp.full((96, 128), faces[r, 2], jnp.int32) == g,
            jnp.full((96, 128), faces[r, 5], jnp.int32) > 0,
        )

    def make_sums(n):
        z = couple([layers[n, (3 + d) * 32 : (4 + d) * 32, :] for d in range(3)])
        z3 = stacked(jnp.concatenate(z, axis=0))
        product = dot(left[1], columns(dot(z3, right[2]), dot(z3, right[3])))
        moved = [jnp.concatenate(planes_of(product, r), axis=0) for r in range(2)]
        for g in (-1, 0, 1):
            total = jnp.where(chosen(0, g), moved[0], 0.0) + jnp.where(chosen(1, g), moved[1], 0.0)
            sums[n, g + 1] = total

    def high_force(n):
        parts = []
        for r in range(2):
            pick = jnp.zeros((96, 128), F32)
            for g in (-1, 0, 1):
                pick = jnp.where(chosen(r, g), low_in[n, g + 1], pick)
            parts.append(dot(stacked(pick), right[r]))
        product = dot(left[0], columns(parts[0], parts[1]))
        a, b = planes_of(product, 0), planes_of(product, 1)
        return couple([x + y for x, y in zip(a, b)])

    def low_force(n):
        total = jnp.zeros((96, 128), F32)
        for g in (-1, 0, 1):
            there = jnp.logical_and(back_ok, side_ok[-g]).astype(jnp.int32)
            total += jnp.where(jnp.full((96, 128), there, jnp.int32) > 0, force_in[n, g + 1], 0.0)
        return total

    def response(force):
        pml = is_pml((PLANE, 128))
        low, high = [], []
        for d in range(3):
            near, far = 0.0, 0.0
            for e in range(3):
                i = PAIRS[(min(d, e), max(d, e))]
                p = misc[ROW_P + i * 32 : ROW_P + (i + 1) * 32, :]
                q = misc[ROW_P + 192 + i * 32 : ROW_P + 192 + (i + 1) * 32, :]
                near = near + (p * force[e] + q * force[3 + e])
                far = far + (q * force[e] + p * force[3 + e])
            low.append(jnp.where(pml, FACE_COEF[d] * force[d], near))
            high.append(jnp.where(pml, FACE_COEF[3 + d] * force[3 + d], far))
        return low + high

    make_sums(0)
    send_ahead(lambda g: force_copy(0, g))
    got_back(flag_copy)

    def theirs(r):
        g = jnp.full((8, 128), faces[r, 2], jnp.int32)
        value = jnp.where(g == -1, flag_in[0], jnp.where(g == 0, flag_in[1], flag_in[2]))
        return jnp.broadcast_to(value[0:1, :], (128, 128))

    their = [theirs(r) for r in range(2)]
    their_col = jnp.where(big_col < 64, their[0], their[1]) > 0.5
    cross_one = jnp.where(their_col, one_pml, one_air)
    left[0] = left_form(cross_one)
    left[1] = left_form(cross_one.T)
    for r in range(2):
        cross_two = jnp.where(their[r] > 0.5, two_pml[r], two_air[r])
        right[r] = right_form(cross_two)
        right[2 + r] = right_form(cross_two.T)
    left[2] = left_form(ours_p)
    right[4] = right_form(ours_t)

    k = big_row.astype(F32)
    rate = 0.5 * ((k + 0.5) * (1.0 / S0)) ** 2
    inverse = 1.0 / (1.0 + rate)
    rows[0] = jnp.where(own, (1.0 - rate) * inverse, 1.0)
    rows[1] = jnp.where(own, (COURANT2 / 90.0) * inverse, 0.0)
    center = (2.0 + COURANT2 * CENTER3) * inverse
    edge = jnp.zeros((S0, 128), F32)
    for b in range(2):
        state[b, :, 0:128] = edge
        state[b, :, 128 + CROSS : 256 + CROSS] = edge
    for c in (0, 1, TILES + 2, TILES + 3):
        rolled[:, c * 128 : (c + 1) * 128] = edge
    pack[192:704, :] = jnp.zeros((512, 128), F32)
    rest[0].wait()

    def tile(c):
        return pl.ds(pl.multiple_of(c * 128, 128), 128)

    @pl.loop(0, TILES)
    def _(c):
        col = c * 128 + big_col
        mode_a = (col >> 6).astype(F32) * (math.pi / S1)
        mode_b = (col & 63).astype(F32) * (math.pi / S2)
        mode_k = k * (math.pi / S0)
        table = gain[:, tile(c)]
        doubled = 2.0 - table * (mode_k * mode_k + mode_a * mode_a + mode_b * mode_b)
        gain[:, tile(c)] = jnp.where(own, 0.0, table)
        slow[:, tile(c)] = jnp.where(own, center, doubled)

    rest[1].wait()
    rest[2].wait()

    alternate = (lax.broadcasted_iota(jnp.int32, (8, 128), 0) & 1) == 0

    def keep_force(force):
        pml = is_pml((PLANE, 128))
        for d in range(3):
            pack[d * 32 : (d + 1) * 32, :] = force[d] + force[3 + d]
            pack[96 + d * 32 : 96 + (d + 1) * 32, :] = force[d] - force[3 + d]
            pack[192 + d * 32 : 192 + (d + 1) * 32, :] = jnp.where(pml, FACE_COEF[d] * force[d], 0.0)
            at = 448 + (7 - d) * 32
            pack[at : at + 32, :] = jnp.where(pml, FACE_COEF[3 + d] * force[3 + d], 0.0)

    def finish(box, table, cut, turn, at, c0, n):
        for h in range(2):
            c = c0 + h
            here = slice(at + h * 128, at + (h + 1) * 128)
            box_here = slice(at + 128 + h * 128, at + 256 + h * 128)
            turn_here = slice(at + 256 + h * 128, at + 384 + h * 128)
            if n > 0:
                mode = mode_rows(pack, alternate, c)
                top = pack[pl.ds(192 + c, 8, stride=PLANE), :]
                bottom = pack[pl.ds(448 + c, 8, stride=PLANE), :]
            for r in range(4):
                row = slice(32 * r, 32 * r + 32)
                block = box[row, box_here]
                if n > 0:
                    block = block + table[row, here] * spread_modes(misc, mode, r)
                    if r == 0:
                        block = jnp.concatenate([block[0:8] + top, block[8:32]], axis=0)
                    if r == 3:
                        block = jnp.concatenate([block[0:24], block[24:32] + bottom], axis=0)
                    box[row, box_here] = block
                hi, lo = split(block)
                cut[row, here] = hi
                cut[slice(128 + 32 * r, 160 + 32 * r), here] = lo
                turn[row, turn_here] = pltpu.roll(block, 64, 1)

    w1, w2 = TAPS_90[0], TAPS_90[1]
    small_first = lax.broadcasted_iota(jnp.int32, (32, 128), 1) < 64

    def advance(b, p, n):
        def step(t, base, with_finish):
            width = 1024 if with_finish else 768
            box = state.at[b, :, pl.ds(base, 896 if with_finish else 512)]
            old = state.at[p, :, pl.ds(base, 512)]
            turn = rolled.at[:, pl.ds(base, width)]
            cut = halved.at[:, pl.ds(base, 768 if with_finish else 256)]
            pair = cut[:, 0:256]
            operand = jnp.concatenate([stencil[0:128, :], pair[0:128, :], pair[128:256, :]], axis=1)
            fixed = stencil[128:384, :]
            taps = dot(operand, jnp.concatenate([pair, fixed, fixed], axis=0))
            if with_finish:
                table = gain.at[:, pl.ds(base, 768)]
                finish(box, table, cut, turn, 512, 2 * t + 4, n)
            own_slow = slow.at[:, pl.ds(base, 256)]
            partial = [None, None]
            ends_ = [[None, None], [None, None]]
            for r in range(4):
                row = slice(32 * r, 32 * r + 32)
                ring = [turn[row, i * 128 : (i + 1) * 128] for i in range(6)]
                line = [box[row, i * 128 : (i + 1) * 128] for i in range(4)]
                quads = [w1 * (ring[i + 2] + ring[i + 1]) + (ring[i + 3] + ring[i]) for i in range(3)]
                for h in range(2):
                    at = slice(h * 128, (h + 1) * 128)
                    total = taps[row, at] + w2 * (line[h] + line[h + 2])
                    total += jnp.where(small_first, quads[h], quads[h + 1])
                    following = own_slow[row, at] * line[h + 1]
                    following -= rows[0, row, :] * old[row, 128 + h * 128 : 256 + h * 128]
                    following += rows[1, row, :] * total
                    old[row, 128 + h * 128 : 256 + h * 128] = following
                    partial[h] = face_part(partial[h], following, r)
                    if r == 0:
                        ends_[h][0] = following[0:8]
                    if r == 3:
                        ends_[h][1] = following[24:32]
            for h in range(2):
                note_faces(partial[h], ends_[h][0], ends_[h][1], 2 * t + h)

        for t in range(2):
            base = t * 256
            finish(
                state.at[b, :, pl.ds(base, 512)], gain.at[:, pl.ds(base, 256)], halved.at[:, pl.ds(base, 256)],
                rolled.at[:, pl.ds(base, 768)], 0, 2 * t, n,
            )

        @pl.loop(0, TILES // 2 - 2)
        def _(t):
            step(t, pl.multiple_of(t * 256, 256), True)

        for t in (TILES // 2 - 2, TILES // 2 - 1):
            step(t, t * 256, False)

        for e, plane in enumerate(gathered_faces()):
            free[e * 32 : (e + 1) * 32, :] = plane

    unforced = pltpu.make_async_copy(
        state.at[STEPS % 2, :, pl.ds(128, CROSS)], free_out, out_sem.at[0]
    )
    for n in range(STEPS):
        b, p = n % 2, 1 - n % 2
        if n > 0:
            send_back(lambda g: low_copy(n, g))
            make_sums(n)
            send_ahead(lambda g: force_copy(n, g))
        advance(b, p, n)
        if n == STEPS - 1:
            unforced.start()
        got_back(lambda g: low_copy(n, g))
        high = high_force(n)
        got_ahead(lambda g: force_copy(n, g))
        low = low_force(n)
        if n == 0:
            turned = dot(stacked(low), right[4])
            low = planes_of(dot(left[2], columns(turned, jnp.zeros((96, 128), F32))), 0)
        else:
            low = [low[e * 32 : (e + 1) * 32, :] for e in range(3)]
        force = low + high
        for e, plane in enumerate(response(force)):
            at = slice(e * 32, (e + 1) * 32)
            layers[n + 1, at, :] = free[at, :] + plane
        keep_force(force)

    pack[704:896, :] = layers[STEPS]
    packed = pltpu.make_async_copy(pack, pack_out, out_sem.at[1])
    packed.start()

    for side, ok in order:

        @pl.when(jnp.logical_and(back_ok, ok))
        def _():
            flag_copy(-side).wait_send()
            for n in range(STEPS):
                low_copy(n, -side).wait_send()

        @pl.when(jnp.logical_and(ahead_ok, ok))
        def _():
            for n in range(STEPS):
                force_copy(n, side).wait_send()

    unforced.wait()
    packed.wait()


def mode_rows(pack, alternate, c):
    out = []
    for d in range(3):
        plus = jnp.broadcast_to(pack[pl.ds(d * 32 + c, 1), :], (8, 128))
        minus = jnp.broadcast_to(pack[pl.ds(96 + d * 32 + c, 1), :], (8, 128))
        out.append(jnp.where(alternate, plus, minus))
    return out


def spread_modes(table, mode, r):
    total = None
    for d in range(3):
        at = ROW_FACE + d * 128 + 32 * r
        term = table[at : at + 32, :].reshape(4, 8, 128) * mode[d][None]
        total = term if total is None else total + term
    return total.reshape(32, 128)


PARTS = 8
WIDE = CROSS // PARTS


def close(flags, pack, misc, free, gain, out, layers_out, done, sems):
    pml = flags[0] > 0
    leave = [
        pltpu.make_async_copy(
            done.at[:, pl.ds(i * WIDE, WIDE)], out.at[0, :, pl.ds(i * WIDE, WIDE)], sems.at[i]
        )
        for i in range(PARTS)
    ]

    @pl.when(pml)
    def _():
        for i in range(PARTS):
            at = slice(i * WIDE, (i + 1) * WIDE)
            done[:, at] = free[:, at]
            for h in range(WIDE // 128):
                c = i * (WIDE // 128) + h
                at = slice(c * 128, (c + 1) * 128)
                done[0:8, at] = free[0:8, at] + pack[pl.ds(192 + c, 8, stride=PLANE), :]
                done[120:128, at] = free[120:128, at] + pack[pl.ds(448 + c, 8, stride=PLANE), :]
            leave[i].start()
        layers_out[...] = pack[704:896, :]

    @pl.when(jnp.logical_not(pml))
    def _():
        alternate = (lax.broadcasted_iota(jnp.int32, (8, 128), 0) & 1) == 0
        for i in range(PARTS):

            @pl.loop(0, WIDE // 256)
            def _(t):
                window = pl.ds(pl.multiple_of(i * WIDE + t * 256, 256), 256)
                source, table, target = free.at[:, window], gain.at[:, window], done.at[:, window]
                for h in range(2):
                    at = slice(h * 128, (h + 1) * 128)
                    mode = mode_rows(pack, alternate, i * (WIDE // 128) + 2 * t + h)
                    for r in range(4):
                        row = slice(32 * r, 32 * r + 32)
                        target[row, at] = source[row, at] + table[row, at] * spread_modes(misc, mode, r)

            leave[i].start()
        turned = dot(stacked(pack[704:896, :]), right_form(misc[ROW_C : ROW_C + 128, :]))
        ours_pt = left_form(misc[ROW_C + 384 : ROW_C + 512, :])
        product = dot(ours_pt, columns(turned[0:96, :], turned[96:192, :]))
        for s in range(2):
            for e, plane in enumerate(planes_of(product, s)):
                at = (3 * s + e) * 32
                layers_out[at : at + 32, :] = plane

    for copy in leave:
        copy.wait()


def local(state_now, state_prev, pml_flags, interfaces):
    gain, misc, stencil = (jnp.asarray(a) for a in constants())
    smem = pl.BlockSpec(memory_space=pltpu.SMEM)
    hbm = pl.BlockSpec(memory_space=pltpu.HBM)
    free, pack = pl.pallas_call(
        exchange,
        out_shape=(
            jax.ShapeDtypeStruct((S0, CROSS), F32),
            jax.ShapeDtypeStruct((896, 128), F32),
        ),
        in_specs=[smem, hbm, hbm, hbm, hbm, hbm, hbm],
        out_specs=(pl.BlockSpec(memory_space=pl.ANY),) * 2,
        scratch_shapes=[
            pltpu.VMEM((2, S0, CROSS + 256), F32),
            pltpu.VMEM((S0, CROSS), F32),
            pltpu.VMEM((S0, CROSS), F32),
            pltpu.VMEM(misc.shape, F32),
            pltpu.VMEM(stencil.shape, BF16),
            pltpu.VMEM((256, CROSS), BF16),
            pltpu.VMEM((S0, CROSS + 512), F32),
            pltpu.VMEM((2, 128, 128), F32),
            pltpu.VMEM((768, 128), F32),
            pltpu.VMEM((512, 128), F32),
            pltpu.VMEM((192, 128), F32),
            pltpu.VMEM((3, 128, 384), BF16),
            pltpu.VMEM((5, 384, 128), BF16),
            pltpu.VMEM((8, 128), F32),
            pltpu.VMEM((3, 8, 128), F32),
            pltpu.VMEM((STEPS + 1, 192, 128), F32),
            pltpu.VMEM((STEPS, 3, 96, 128), F32),
            pltpu.VMEM((STEPS, 3, 96, 128), F32),
            pltpu.VMEM((STEPS, 3, 96, 128), F32),
            pltpu.VMEM((896, 128), F32),
            pltpu.SMEM((2, 6), jnp.int32),
            pltpu.SemaphoreType.DMA((9,)),
            pltpu.SemaphoreType.DMA((21,)),
            pltpu.SemaphoreType.DMA((21,)),
            pltpu.SemaphoreType.DMA((2,)),
        ],
        compiler_params=pltpu.CompilerParams(
            collective_id=0, has_side_effects=True, vmem_limit_bytes=32 * 1024 * 1024
        ),
    )(
        pml_flags,
        *(
            pltpu.with_memory_space_constraint(x, pltpu.HBM)
            for x in (interfaces, state_now, state_prev, gain, misc, stencil)
        ),
    )

    whole = pl.BlockSpec(memory_space=pltpu.VMEM)
    new_state, planes = pl.pallas_call(
        close,
        out_shape=(
            jax.ShapeDtypeStruct((1, S0, CROSS), F32),
            jax.ShapeDtypeStruct((192, 128), F32),
        ),
        in_specs=[smem, whole, whole, whole, whole],
        out_specs=(hbm, whole),
        scratch_shapes=[pltpu.VMEM((S0, CROSS), F32), pltpu.SemaphoreType.DMA((PARTS,))],
        compiler_params=pltpu.CompilerParams(vmem_limit_bytes=24 * 1024 * 1024),
    )(pml_flags, pack, misc, free, gain)
    return new_state, planes.reshape(1, 6, CROSS)


def solution(mesh):
    one, two, three = P(("gx", "gy")), P(("gx", "gy"), None), P(("gx", "gy"), None, None)
    return jax.shard_map(
        local,
        mesh=mesh,
        in_specs=(three, three, one, two),
        out_specs=(three, three),
        check_vma=False,
    )
```

time: 46.7 us -> 32.6 us (0.70)
  the two profiles are of different devices: /device:TPU:55 before, /device:TPU:57 now
where the time goes in v1:
time: 32.6 us; the launch traced here: 32.5 us
  Pallas kernels  31.2 us (96%)
  between operations  1.32 us (4%)
    pallas_call x1, Pallas kernels, local(): pl.pallas_call(exchange, out_shape=(jax.ShapeDtypeStruct((S0, CROSS), F32...  29 us
    pallas_call x1, Pallas kernels, local(): pl.pallas_call(close, out_shape=(jax.ShapeDtypeStruct((1, S0, CROSS), F32...  2.22 us

profile of v1, /device:TPU:57, one launch (start us, length us, event | category | flops | bytes accessed | tf_op | source)
XLA Modules:
  0.0 32.5 jit_solution(635391662832199225)
XLA Ops:
  1.3 0.0 copy-start
  1.3 0.0 copy-start.1
  1.3 29.0 %shard_map.86 = (f32[128,4096]{1,0:T(8,128)S(1)}, f32[896,128]{1,0:T(8,128)S(1)}) custom-call(s32[1]{0:T(128)S(6)} %copy.11.flags, s32[2,6]{1,0:T(2,128)} %faces_hbm.1, f32[1,128,4096]{2,1,0:T(8,128)} %now_hbm.1, f32[1,128,4096]{2,1,0:T(8,128)} %prev_hbm.1, f32[128,4096]{1,0:T(8,128)} %constant.6.clone.gain_hbm.gain, ...), custom_call_target="tpu_custom_call" | custom-call | tf_op jit(solution)/shard_map/pallas_call | solution.py:664
  30.3 0.0 copy-done
  30.3 0.0 copy-done.1
  30.3 2.2 %shard_map.87 = (f32[1,128,4096]{2,1,0:T(8,128)}, f32[192,128]{1,0:T(8,128)}) custom-call(s32[1]{0:T(128)S(6)} %copy.11.flags, f32[896,128]{1,0:T(8,128)S(1)} %get-tuple-element.6.pack, f32[1280,128]{1,0:T(8,128)S(1)} %copy-done.1, f32[128,4096]{1,0:T(8,128)S(1)} %get-tuple-element.7.free, f32[128,4096]{1,0:T(8,128)S(1)} %copy-done), custom_call_target="tpu_custom_call" | custom-call | tf_op jit(solution)/shard_map/pallas_call | solution.py:711
Async XLA Ops:
  1.3 29.0 %copy-start = (f32[128,4096]{1,0:T(8,128)S(1)}, f32[128,4096]{1,0:T(8,128)}, u32[]{:S(2)}) copy-start(f32[128,4096]{1,0:T(8,128)} %constant.6.clone.gain_hbm.gain) | copy-start | bytes 6291460
  1.3 29.0 %copy-start.1 = (f32[1280,128]{1,0:T(8,128)S(1)}, f32[1280,128]{1,0:T(8,128)}, u32[]{:S(2)}) copy-start(f32[1280,128]{1,0:T(8,128)} %constant.7.clone.misc_hbm.misc) | copy-start | bytes 1966084

commit v2 on v1

--- a/solution.py
+++ b/solution.py
@@ -71,7 +71,12 @@
 
     along = band(S0)
     stencil = np.concatenate([np.concatenate([along, along], axis=1), twice(twice(band(S2)))], axis=0)
-    return gain.astype(np.float32), misc.astype(np.float32), stencil.astype(BF16)
+    six = np.zeros((S0, 8))
+    six[:, 0:6] = c0[:, [0, 1, 2, 127, 126, 125]]
+    high = six.astype(np.float32).astype(BF16)
+    low = (six - high.astype(np.float64)).astype(np.float32).astype(BF16)
+    modes = np.concatenate([high, high, low, np.zeros((S0, 8), BF16)], axis=1)
+    return gain.astype(np.float32), misc.astype(np.float32), stencil.astype(BF16), modes
 
 
 ROW_FACE, ROW_P, ROW_C = 0, 384, 768
@@ -144,9 +149,9 @@
 
 
 def exchange(
-    flags, faces_hbm, now_hbm, prev_hbm, gain_hbm, misc_hbm, stencil_hbm,
+    flags, faces_hbm, now_hbm, prev_hbm, gain_hbm, misc_hbm, stencil_hbm, modes_hbm,
     free_out, pack_out,
-    state, gain, slow, misc, stencil, halved, rolled, rows,
+    state, gain, slow, misc, modes, stencil, halved, rolled, tapped, rows,
     acc, picked, free, left, right, flag_out, flag_in, layers, sums, low_in, force_in, pack,
     faces, load_sem, send_sem, recv_sem, out_sem,
 ):
@@ -182,6 +187,7 @@
         pltpu.make_async_copy(gain_hbm, gain, load_sem.at[1]),
         pltpu.make_async_copy(prev_hbm.at[0], state.at[1, :, pl.ds(128, CROSS)], load_sem.at[2]),
         pltpu.make_async_copy(stencil_hbm, stencil, load_sem.at[3]),
+        pltpu.make_async_copy(modes_hbm, modes, load_sem.at[9]),
     ]
     for load in rest:
         load.start()
@@ -391,38 +397,20 @@
 
     make_sums(0)
     send_ahead(lambda g: force_copy(0, g))
-    got_back(flag_copy)
-
-    def theirs(r):
-        g = jnp.full((8, 128), faces[r, 2], jnp.int32)
-        value = jnp.where(g == -1, flag_in[0], jnp.where(g == 0, flag_in[1], flag_in[2]))
-        return jnp.broadcast_to(value[0:1, :], (128, 128))
-
-    their = [theirs(r) for r in range(2)]
-    their_col = jnp.where(big_col < 64, their[0], their[1]) > 0.5
-    cross_one = jnp.where(their_col, one_pml, one_air)
-    left[0] = left_form(cross_one)
-    left[1] = left_form(cross_one.T)
-    for r in range(2):
-        cross_two = jnp.where(their[r] > 0.5, two_pml[r], two_air[r])
-        right[r] = right_form(cross_two)
-        right[2 + r] = right_form(cross_two.T)
-    left[2] = left_form(ours_p)
-    right[4] = right_form(ours_t)
-
     k = big_row.astype(F32)
     rate = 0.5 * ((k + 0.5) * (1.0 / S0)) ** 2
     inverse = 1.0 / (1.0 + rate)
     rows[0] = jnp.where(own, (1.0 - rate) * inverse, 1.0)
     rows[1] = jnp.where(own, (COURANT2 / 90.0) * inverse, 0.0)
     center = (2.0 + COURANT2 * CENTER3) * inverse
+    mode_k = (k * (math.pi / S0)) * (k * (math.pi / S0))
     edge = jnp.zeros((S0, 128), F32)
     for b in range(2):
         state[b, :, 0:128] = edge
         state[b, :, 128 + CROSS : 256 + CROSS] = edge
     for c in (0, 1, TILES + 2, TILES + 3):
         rolled[:, c * 128 : (c + 1) * 128] = edge
-    pack[192:704, :] = jnp.zeros((512, 128), F32)
+    pack[192:768, :] = jnp.zeros((576, 128), F32)
     rest[0].wait()
 
     def tile(c):
@@ -430,48 +418,44 @@
 
     @pl.loop(0, TILES)
     def _(c):
-        col = c * 128 + big_col
+        col = c * 128 + lax.broadcasted_iota(jnp.int32, (1, 128), 1)
         mode_a = (col >> 6).astype(F32) * (math.pi / S1)
         mode_b = (col & 63).astype(F32) * (math.pi / S2)
-        mode_k = k * (math.pi / S0)
-        table = gain[:, tile(c)]
-        doubled = 2.0 - table * (mode_k * mode_k + mode_a * mode_a + mode_b * mode_b)
-        gain[:, tile(c)] = jnp.where(own, 0.0, table)
-        slow[:, tile(c)] = jnp.where(own, center, doubled)
+        wave = mode_k + (mode_a * mode_a + mode_b * mode_b)
+        slow[:, tile(c)] = jnp.where(own, center, 2.0 - gain[:, tile(c)] * wave)
 
     rest[1].wait()
     rest[2].wait()
-
-    alternate = (lax.broadcasted_iota(jnp.int32, (8, 128), 0) & 1) == 0
+    rest[3].wait()
 
     def keep_force(force):
         pml = is_pml((PLANE, 128))
         for d in range(3):
-            pack[d * 32 : (d + 1) * 32, :] = force[d] + force[3 + d]
-            pack[96 + d * 32 : 96 + (d + 1) * 32, :] = force[d] - force[3 + d]
-            pack[192 + d * 32 : 192 + (d + 1) * 32, :] = jnp.where(pml, FACE_COEF[d] * force[d], 0.0)
-            at = 448 + (7 - d) * 32
+            pack[d * 32 : (d + 1) * 32, :] = jnp.where(pml, 0.0, force[d])
+            pack[96 + d * 32 : 96 + (d + 1) * 32, :] = jnp.where(pml, 0.0, force[3 + d])
+            pack[256 + d * 32 : 256 + (d + 1) * 32, :] = jnp.where(pml, FACE_COEF[d] * force[d], 0.0)
+            at = 512 + (7 - d) * 32
             pack[at : at + 32, :] = jnp.where(pml, FACE_COEF[3 + d] * force[3 + d], 0.0)
 
     def finish(box, table, cut, turn, at, c0, n):
-        for h in range(2):
-            c = c0 + h
-            here = slice(at + h * 128, at + (h + 1) * 128)
-            box_here = slice(at + 128 + h * 128, at + 256 + h * 128)
-            turn_here = slice(at + 256 + h * 128, at + 384 + h * 128)
-            if n > 0:
-                mode = mode_rows(pack, alternate, c)
-                top = pack[pl.ds(192 + c, 8, stride=PLANE), :]
-                bottom = pack[pl.ds(448 + c, 8, stride=PLANE), :]
-            for r in range(4):
-                row = slice(32 * r, 32 * r + 32)
+        if n > 0:
+            along_box = spread_modes(modes, pack, c0)
+            top = both(pack, 256, c0)
+            bottom = both(pack, 512, c0)
+        for r in range(4):
+            row = slice(32 * r, 32 * r + 32)
+            for h in range(2):
+                here = slice(at + h * 128, at + (h + 1) * 128)
+                box_here = slice(at + 128 + h * 128, at + 256 + h * 128)
+                turn_here = slice(at + 256 + h * 128, at + 384 + h * 128)
+                side = slice(h * 128, (h + 1) * 128)
                 block = box[row, box_here]
                 if n > 0:
-                    block = block + table[row, here] * spread_modes(misc, mode, r)
+                    block = block + table[row, here] * along_box[row, side]
                     if r == 0:
-                        block = jnp.concatenate([block[0:8] + top, block[8:32]], axis=0)
+                        block = jnp.concatenate([block[0:8] + top[:, side], block[8:32]], axis=0)
                     if r == 3:
-                        block = jnp.concatenate([block[0:24], block[24:32] + bottom], axis=0)
+                        block = jnp.concatenate([block[0:24], block[24:32] + bottom[:, side]], axis=0)
                     box[row, box_here] = block
                 hi, lo = split(block)
                 cut[row, here] = hi
@@ -481,43 +465,47 @@
     w1, w2 = TAPS_90[0], TAPS_90[1]
     small_first = lax.broadcasted_iota(jnp.int32, (32, 128), 1) < 64
 
+    def keep_taps(cut, at, slot):
+        pair = cut[:, at : at + 256]
+        operand = jnp.concatenate([stencil[0:128, :], pair[0:128, :], pair[128:256, :]], axis=1)
+        fixed = stencil[128:384, :]
+        tapped[slot] = dot(operand, jnp.concatenate([pair, fixed, fixed], axis=0))
+
     def advance(b, p, n):
-        def step(t, base, with_finish):
-            width = 1024 if with_finish else 768
-            box = state.at[b, :, pl.ds(base, 896 if with_finish else 512)]
-            old = state.at[p, :, pl.ds(base, 512)]
-            turn = rolled.at[:, pl.ds(base, width)]
-            cut = halved.at[:, pl.ds(base, 768 if with_finish else 256)]
-            pair = cut[:, 0:256]
-            operand = jnp.concatenate([stencil[0:128, :], pair[0:128, :], pair[128:256, :]], axis=1)
-            fixed = stencil[128:384, :]
-            taps = dot(operand, jnp.concatenate([pair, fixed, fixed], axis=0))
-            if with_finish:
-                table = gain.at[:, pl.ds(base, 768)]
-                finish(box, table, cut, turn, 512, 2 * t + 4, n)
-            own_slow = slow.at[:, pl.ds(base, 256)]
+        def step(base, c0, at, slot, ahead_by, width):
+            box = state.at[b, :, pl.ds(base, 256 + width)]
+            old = state.at[p, :, pl.ds(base, 256 + width)]
+            turn = rolled.at[:, pl.ds(base, 512 + width)]
+            cut = halved.at[:, pl.ds(base, width)]
+            table = gain.at[:, pl.ds(base, width)]
+            own_slow = slow.at[:, pl.ds(base, width)]
+            if ahead_by > 0:
+                keep_taps(cut, at + 256, 1 - slot)
+            if ahead_by > 1:
+                finish(box, table, cut, turn, at + 512, c0 + 4, n)
             partial = [None, None]
             ends_ = [[None, None], [None, None]]
             for r in range(4):
                 row = slice(32 * r, 32 * r + 32)
-                ring = [turn[row, i * 128 : (i + 1) * 128] for i in range(6)]
-                line = [box[row, i * 128 : (i + 1) * 128] for i in range(4)]
+                ring = [turn[row, at + i * 128 : at + (i + 1) * 128] for i in range(6)]
+                line = [box[row, at + i * 128 : at + (i + 1) * 128] for i in range(4)]
                 quads = [w1 * (ring[i + 2] + ring[i + 1]) + (ring[i + 3] + ring[i]) for i in range(3)]
                 for h in range(2):
-                    at = slice(h * 128, (h + 1) * 128)
-                    total = taps[row, at] + w2 * (line[h] + line[h + 2])
+                    here = slice(at + h * 128, at + (h + 1) * 128)
+                    box_here = slice(at + 128 + h * 128, at + 256 + h * 128)
+                    total = tapped[slot, row, h * 128 : (h + 1) * 128] + w2 * (line[h] + line[h + 2])
                     total += jnp.where(small_first, quads[h], quads[h + 1])
-                    following = own_slow[row, at] * line[h + 1]
-                    following -= rows[0, row, :] * old[row, 128 + h * 128 : 256 + h * 128]
+                    following = own_slow[row, here] * line[h + 1]
+                    following -= rows[0, row, :] * old[row, box_here]
                     following += rows[1, row, :] * total
-                    old[row, 128 + h * 128 : 256 + h * 128] = following
+                    old[row, box_here] = following
                     partial[h] = face_part(partial[h], following, r)
                     if r == 0:
                         ends_[h][0] = following[0:8]
                     if r == 3:
                         ends_[h][1] = following[24:32]
             for h in range(2):
-                note_faces(partial[h], ends_[h][0], ends_[h][1], 2 * t + h)
+                note_faces(partial[h], ends_[h][0], ends_[h][1], c0 + h)
 
         for t in range(2):
             base = t * 256
@@ -525,16 +513,39 @@
                 state.at[b, :, pl.ds(base, 512)], gain.at[:, pl.ds(base, 256)], halved.at[:, pl.ds(base, 256)],
                 rolled.at[:, pl.ds(base, 768)], 0, 2 * t, n,
             )
-
-        @pl.loop(0, TILES // 2 - 2)
-        def _(t):
-            step(t, pl.multiple_of(t * 256, 256), True)
-
-        for t in (TILES // 2 - 2, TILES // 2 - 1):
-            step(t, t * 256, False)
+        keep_taps(halved, 0, 0)
+
+        @pl.loop(0, TILES // 4 - 1)
+        def _(i):
+            base = pl.multiple_of(i * 512, 512)
+            for s in range(2):
+                step(base, 4 * i + 2 * s, 256 * s, s, 2, 1024)
+
+        base = CROSS - 512
+        step(base, TILES - 4, 0, 0, 1, 512)
+        step(base, TILES - 2, 256, 1, 0, 512)
 
         for e, plane in enumerate(gathered_faces()):
             free[e * 32 : (e + 1) * 32, :] = plane
+
+    def theirs(r):
+        g = jnp.full((8, 128), faces[r, 2], jnp.int32)
+        value = jnp.where(g == -1, flag_in[0], jnp.where(g == 0, flag_in[1], flag_in[2]))
+        return jnp.broadcast_to(value[0:1, :], (128, 128))
+
+    def finish_matrices():
+        got_back(flag_copy)
+        their = [theirs(r) for r in range(2)]
+        their_col = jnp.where(big_col < 64, their[0], their[1]) > 0.5
+        cross_one = jnp.where(their_col, one_pml, one_air)
+        left[0] = left_form(cross_one)
+        left[1] = left_form(cross_one.T)
+        for r in range(2):
+            cross_two = jnp.where(their[r] > 0.5, two_pml[r], two_air[r])
+            right[r] = right_form(cross_two)
+            right[2 + r] = right_form(cross_two.T)
+        left[2] = left_form(ours_p)
+        right[4] = right_form(ours_t)
 
     unforced = pltpu.make_async_copy(
         state.at[STEPS % 2, :, pl.ds(128, CROSS)], free_out, out_sem.at[0]
@@ -545,7 +556,10 @@
             send_back(lambda g: low_copy(n, g))
             make_sums(n)
             send_ahead(lambda g: force_copy(n, g))
+            keep_force(force)
         advance(b, p, n)
+        if n == 0:
+            finish_matrices()
         if n == STEPS - 1:
             unforced.start()
         got_back(lambda g: low_copy(n, g))
@@ -561,9 +575,9 @@
         for e, plane in enumerate(response(force)):
             at = slice(e * 32, (e + 1) * 32)
             layers[n + 1, at, :] = free[at, :] + plane
-        keep_force(force)
-
-    pack[704:896, :] = layers[STEPS]
+
+    keep_force(force)
+    pack[768:960, :] = layers[STEPS]
     packed = pltpu.make_async_copy(pack, pack_out, out_sem.at[1])
     packed.start()
 
@@ -584,22 +598,15 @@
     packed.wait()
 
 
-def mode_rows(pack, alternate, c):
-    out = []
-    for d in range(3):
-        plus = jnp.broadcast_to(pack[pl.ds(d * 32 + c, 1), :], (8, 128))
-        minus = jnp.broadcast_to(pack[pl.ds(96 + d * 32 + c, 1), :], (8, 128))
-        out.append(jnp.where(alternate, plus, minus))
-    return out
-
-
-def spread_modes(table, mode, r):
-    total = None
-    for d in range(3):
-        at = ROW_FACE + d * 128 + 32 * r
-        term = table[at : at + 32, :].reshape(4, 8, 128) * mode[d][None]
-        total = term if total is None else total + term
-    return total.reshape(32, 128)
+def both(pack, row, c):
+    return jnp.concatenate([pack[pl.ds(row + c + h, 8, stride=PLANE), :] for h in range(2)], axis=1)
+
+
+def spread_modes(modes, pack, c):
+    hi, lo = split(both(pack, 0, c))
+    hi = hi.astype(F32)
+    terms = jnp.concatenate([hi, lo.astype(F32), hi, jnp.zeros((8, 256), F32)], axis=0)
+    return dot(modes[...], terms.astype(BF16))
 
 
 PARTS = 8
@@ -623,14 +630,14 @@
             for h in range(WIDE // 128):
                 c = i * (WIDE // 128) + h
                 at = slice(c * 128, (c + 1) * 128)
-                done[0:8, at] = free[0:8, at] + pack[pl.ds(192 + c, 8, stride=PLANE), :]
-                done[120:128, at] = free[120:128, at] + pack[pl.ds(448 + c, 8, stride=PLANE), :]
+                done[0:8, at] = free[0:8, at] + pack[pl.ds(256 + c, 8, stride=PLANE), :]
+                done[120:128, at] = free[120:128, at] + pack[pl.ds(512 + c, 8, stride=PLANE), :]
             leave[i].start()
-        layers_out[...] = pack[704:896, :]
+        layers_out[...] = pack[768:960, :]
 
     @pl.when(jnp.logical_not(pml))
     def _():
-        alternate = (lax.broadcasted_iota(jnp.int32, (8, 128), 0) & 1) == 0
+        even = (lax.broadcasted_iota(jnp.int32, (8, 128), 0) & 1) == 0
         for i in range(PARTS):
 
             @pl.loop(0, WIDE // 256)
@@ -639,13 +646,23 @@
                 source, table, target = free.at[:, window], gain.at[:, window], done.at[:, window]
                 for h in range(2):
                     at = slice(h * 128, (h + 1) * 128)
-                    mode = mode_rows(pack, alternate, i * (WIDE // 128) + 2 * t + h)
+                    c = i * (WIDE // 128) + 2 * t + h
+                    mode = []
+                    for d in range(3):
+                        low = jnp.broadcast_to(pack[pl.ds(d * 32 + c, 1), :], (8, 128))
+                        high = jnp.broadcast_to(pack[pl.ds(96 + d * 32 + c, 1), :], (8, 128))
+                        mode.append(low + jnp.where(even, high, -high))
                     for r in range(4):
                         row = slice(32 * r, 32 * r + 32)
-                        target[row, at] = source[row, at] + table[row, at] * spread_modes(misc, mode, r)
+                        total = None
+                        for d in range(3):
+                            at_d = ROW_FACE + d * 128 + 32 * r
+                            term = misc[at_d : at_d + 32, :].reshape(4, 8, 128) * mode[d][None]
+                            total = term if total is None else total + term
+                        target[row, at] = source[row, at] + table[row, at] * total.reshape(32, 128)
 
             leave[i].start()
-        turned = dot(stacked(pack[704:896, :]), right_form(misc[ROW_C : ROW_C + 128, :]))
+        turned = dot(stacked(pack[768:960, :]), right_form(misc[ROW_C : ROW_C + 128, :]))
         ours_pt = left_form(misc[ROW_C + 384 : ROW_C + 512, :])
         product = dot(ours_pt, columns(turned[0:96, :], turned[96:192, :]))
         for s in range(2):
@@ -658,25 +675,28 @@
 
 
 def local(state_now, state_prev, pml_flags, interfaces):
-    gain, misc, stencil = (jnp.asarray(a) for a in constants())
+    gain, misc, stencil, modes = (jnp.asarray(a) for a in constants())
     smem = pl.BlockSpec(memory_space=pltpu.SMEM)
+    whole = pl.BlockSpec(memory_space=pltpu.VMEM)
     hbm = pl.BlockSpec(memory_space=pltpu.HBM)
     free, pack = pl.pallas_call(
         exchange,
         out_shape=(
             jax.ShapeDtypeStruct((S0, CROSS), F32),
-            jax.ShapeDtypeStruct((896, 128), F32),
+            jax.ShapeDtypeStruct((960, 128), F32),
         ),
-        in_specs=[smem, hbm, hbm, hbm, hbm, hbm, hbm],
+        in_specs=[smem] + [hbm] * 7,
         out_specs=(pl.BlockSpec(memory_space=pl.ANY),) * 2,
         scratch_shapes=[
             pltpu.VMEM((2, S0, CROSS + 256), F32),
             pltpu.VMEM((S0, CROSS), F32),
             pltpu.VMEM((S0, CROSS), F32),
             pltpu.VMEM(misc.shape, F32),
+            pltpu.VMEM(modes.shape, BF16),
             pltpu.VMEM(stencil.shape, BF16),
             pltpu.VMEM((256, CROSS), BF16),
             pltpu.VMEM((S0, CROSS + 512), F32),
+            pltpu.VMEM((2, 128, 256), F32),
             pltpu.VMEM((2, 128, 128), F32),
             pltpu.VMEM((768, 128), F32),
             pltpu.VMEM((512, 128), F32),
@@ -689,9 +709,9 @@
             pltpu.VMEM((STEPS, 3, 96, 128), F32),
             pltpu.VMEM((STEPS, 3, 96, 128), F32),
             pltpu.VMEM((STEPS, 3, 96, 128), F32),
-            pltpu.VMEM((896, 128), F32),
+            pltpu.VMEM((960, 128), F32),
             pltpu.SMEM((2, 6), jnp.int32),
-            pltpu.SemaphoreType.DMA((9,)),
+            pltpu.SemaphoreType.DMA((10,)),
             pltpu.SemaphoreType.DMA((21,)),
             pltpu.SemaphoreType.DMA((21,)),
             pltpu.SemaphoreType.DMA((2,)),
@@ -703,18 +723,17 @@
         pml_flags,
         *(
             pltpu.with_memory_space_constraint(x, pltpu.HBM)
-            for x in (interfaces, state_now, state_prev, gain, misc, stencil)
+            for x in (interfaces, state_now, state_prev, gain, misc, stencil, modes)
         ),
     )
 
-    whole = pl.BlockSpec(memory_space=pltpu.VMEM)
     new_state, planes = pl.pallas_call(
         close,
         out_shape=(
             jax.ShapeDtypeStruct((1, S0, CROSS), F32),
             jax.ShapeDtypeStruct((192, 128), F32),
         ),
-        in_specs=[smem, whole, whole, whole, whole],
+        in_specs=[smem] + [whole] * 4,
         out_specs=(hbm, whole),
         scratch_shapes=[pltpu.VMEM((S0, CROSS), F32), pltpu.SemaphoreType.DMA((PARTS,))],
         compiler_params=pltpu.CompilerParams(vmem_limit_bytes=24 * 1024 * 1024),

time: 32.6 us -> 29.3 us (0.90)
  Pallas kernels: 31.2 us -> 27.6 us
    pallas_call x1, Pallas kernels: 29 us -> 25.5 us  [local(): pl.pallas_call(exchange, out_shape=(jax.ShapeDtypeStruct((S0, CROSS), F32...]
where the time goes in v2:
time: 29.3 us; the launch traced here: 28.9 us
  Pallas kernels  27.6 us (94%)
  between operations  1.32 us (5%)
    pallas_call x1, Pallas kernels, local(): pl.pallas_call(exchange, out_shape=(jax.ShapeDtypeStruct((S0, CROSS), F32...  25.5 us
    pallas_call x1, Pallas kernels, local(): pl.pallas_call(close, out_shape=(jax.ShapeDtypeStruct((1, S0, CROSS), F32...  2.06 us

profile of v2, /device:TPU:57, one launch (start us, length us, event | category | flops | bytes accessed | tf_op | source)
XLA Modules:
  0.0 28.9 jit_solution(9306892447403679899)
XLA Ops:
  1.3 0.0 copy-start
  1.3 0.0 copy-start.1
  1.3 25.5 %shard_map.95 = (f32[128,4096]{1,0:T(8,128)S(1)}, f32[960,128]{1,0:T(8,128)S(1)}) custom-call(s32[1]{0:T(128)S(6)} %copy.12.flags, s32[2,6]{1,0:T(2,128)} %faces_hbm.1, f32[1,128,4096]{2,1,0:T(8,128)} %now_hbm.1, f32[1,128,4096]{2,1,0:T(8,128)} %prev_hbm.1, f32[128,4096]{1,0:T(8,128)} %constant.8.clone.gain_hbm.gain, ...), custom_call_target="tpu_custom_call" | custom-call | tf_op jit(solution)/shard_map/pallas_call | solution.py:682
  26.8 0.0 copy-done
  26.8 0.0 copy-done.1
  26.9 2.1 %shard_map.96 = (f32[1,128,4096]{2,1,0:T(8,128)}, f32[192,128]{1,0:T(8,128)}) custom-call(s32[1]{0:T(128)S(6)} %copy.12.flags, f32[960,128]{1,0:T(8,128)S(1)} %get-tuple-element.6.pack, f32[1280,128]{1,0:T(8,128)S(1)} %copy-done.1, f32[128,4096]{1,0:T(8,128)S(1)} %get-tuple-element.7.free, f32[128,4096]{1,0:T(8,128)S(1)} %copy-done), custom_call_target="tpu_custom_call" | custom-call | tf_op jit(solution)/shard_map/pallas_call | solution.py:730
Async XLA Ops:
  1.3 25.6 %copy-start = (f32[128,4096]{1,0:T(8,128)S(1)}, f32[128,4096]{1,0:T(8,128)}, u32[]{:S(2)}) copy-start(f32[128,4096]{1,0:T(8,128)} %constant.8.clone.gain_hbm.gain) | copy-start | bytes 6291460
  1.3 25.6 %copy-start.1 = (f32[1280,128]{1,0:T(8,128)S(1)}, f32[1280,128]{1,0:T(8,128)}, u32[]{:S(2)}) copy-start(f32[1280,128]{1,0:T(8,128)} %constant.9.clone.misc_hbm.misc) | copy-start | bytes 1966084

commit v3 on v2

--- a/solution.py
+++ b/solution.py
@@ -157,16 +157,6 @@
 ):
     gx, gy = lax.axis_index("gx"), lax.axis_index("gy")
     nx, ny = lax.axis_size("gx"), lax.axis_size("gy")
-
-    back_ok, ahead_ok = gx > 0, gx < nx - 1
-    side_ok = {-1: gy > 0, 0: gy >= 0, 1: gy < ny - 1}
-    barrier = pltpu.get_barrier_semaphore()
-    for ok, to_x in ((back_ok, gx - 1), (ahead_ok, gx + 1)):
-        for side in (-1, 0, 1):
-
-            @pl.when(jnp.logical_and(ok, side_ok[side]))
-            def _():
-                pl.semaphore_signal(barrier, inc=1, device_id=(to_x, gy + side), device_id_type=MESH)
 
     head = pltpu.make_async_copy(misc_hbm, misc, load_sem.at[0])
     head.start()
@@ -191,6 +181,16 @@
     ]
     for load in rest:
         load.start()
+    back_ok, ahead_ok = gx > 0, gx < nx - 1
+    side_ok = {-1: gy > 0, 0: gy >= 0, 1: gy < ny - 1}
+    barrier = pltpu.get_barrier_semaphore()
+    for ok, to_x in ((back_ok, gx - 1), (ahead_ok, gx + 1)):
+        for side in (-1, 0, 1):
+
+            @pl.when(jnp.logical_and(ok, side_ok[side]))
+            def _():
+                pl.semaphore_signal(barrier, inc=1, device_id=(to_x, gy + side), device_id_type=MESH)
+
     flag_out[...] = jnp.full(flag_out.shape, flags[0], jnp.int32).astype(F32)
 
     core = lax.rem(gy, 2)
@@ -301,11 +301,16 @@
     pl.semaphore_wait(barrier, sides * ends)
     send_back(flag_copy)
 
+    line = lax.broadcasted_iota(jnp.int32, (8, 128), 0)
+
     def note_faces(partial, top, bottom, c):
+        full = []
         for d in range(3):
-            acc[pl.ds(d * 256 + c, 8, stride=PLANE), :] = partial[d]
-        picked[pl.ds(c, 8, stride=PLANE), :] = top
-        picked[pl.ds(256 + c, 8, stride=PLANE), :] = bottom
+            v = partial[d] + pltpu.roll(partial[d], 4, 0)
+            full.append(v + pltpu.roll(v, 2, 0))
+        at = pl.ds(pl.multiple_of(c * 8, 8), 8)
+        acc[at, :] = jnp.where(line < 2, full[0], jnp.where(line < 4, full[1], full[2]))
+        picked[at, :] = jnp.where(line < 4, top, bottom)
 
     def face_part(partial, chunk_rows, r):
         tiles = chunk_rows.reshape(4, 8, 128)
@@ -321,11 +326,10 @@
         low, high = [], []
         pml = is_pml((PLANE, 128))
         for d in range(3):
-            part = [acc[d * 256 + s * 32 : d * 256 + (s + 1) * 32, :] for s in range(8)]
-            even = (part[0] + part[2]) + (part[4] + part[6])
-            odd = (part[1] + part[3]) + (part[5] + part[7])
-            row_low = picked[d * 32 : (d + 1) * 32, :]
-            row_high = picked[256 + (7 - d) * 32 : 256 + (8 - d) * 32, :]
+            even = acc[pl.ds(2 * d, PLANE, stride=8), :]
+            odd = acc[pl.ds(2 * d + 1, PLANE, stride=8), :]
+            row_low = picked[pl.ds(d, PLANE, stride=8), :]
+            row_high = picked[pl.ds(7 - d, PLANE, stride=8), :]
             low.append(jnp.where(pml, row_low, even + odd))
             high.append(jnp.where(pml, row_high, even - odd))
         return low + high
@@ -336,12 +340,13 @@
         @pl.loop(0, TILES // 8)
         def _(t):
             window = state.at[0, :, pl.ds(pl.multiple_of(128 + i * chunk + t * 256, 128), 256)]
+            ats = [slice(h * 128, (h + 1) * 128) for h in range(2)]
+            partial = [None, None]
+            for r in range(4):
+                for h in range(2):
+                    partial[h] = face_part(partial[h], window[32 * r : 32 * r + 32, ats[h]], r)
             for h in range(2):
-                at = slice(h * 128, (h + 1) * 128)
-                partial = None
-                for r in range(4):
-                    partial = face_part(partial, window[32 * r : 32 * r + 32, at], r)
-                note_faces(partial, window[0:8, at], window[120:128, at], 8 * i + 2 * t + h)
+                note_faces(partial[h], window[0:8, ats[h]], window[120:128, ats[h]], 8 * i + 2 * t + h)
 
     for e, plane in enumerate(gathered_faces()):
         layers[0, e * 32 : (e + 1) * 32, :] = plane
@@ -644,22 +649,25 @@
             def _(t):
                 window = pl.ds(pl.multiple_of(i * WIDE + t * 256, 256), 256)
                 source, table, target = free.at[:, window], gain.at[:, window], done.at[:, window]
+                modes = []
                 for h in range(2):
-                    at = slice(h * 128, (h + 1) * 128)
                     c = i * (WIDE // 128) + 2 * t + h
                     mode = []
                     for d in range(3):
                         low = jnp.broadcast_to(pack[pl.ds(d * 32 + c, 1), :], (8, 128))
                         high = jnp.broadcast_to(pack[pl.ds(96 + d * 32 + c, 1), :], (8, 128))
                         mode.append(low + jnp.where(even, high, -high))
-                    for r in range(4):
-                        row = slice(32 * r, 32 * r + 32)
-                        total = None
-                        for d in range(3):
-                            at_d = ROW_FACE + d * 128 + 32 * r
-                            term = misc[at_d : at_d + 32, :].reshape(4, 8, 128) * mode[d][None]
-                            total = term if total is None else total + term
-                        target[row, at] = source[row, at] + table[row, at] * total.reshape(32, 128)
+                    modes.append(mode)
+                for r in range(8):
+                    row = slice(16 * r, 16 * r + 16)
+                    weights = [
+                        misc[ROW_FACE + d * 128 + 16 * r : ROW_FACE + d * 128 + 16 * r + 16, :].reshape(2, 8, 128)
+                        for d in range(3)
+                    ]
+                    for h in range(2):
+                        at = slice(h * 128, (h + 1) * 128)
+                        total = sum(weights[d] * modes[h][d][None] for d in range(3))
+                        target[row, at] = source[row, at] + table[row, at] * total.reshape(16, 128)
 
             leave[i].start()
         turned = dot(stacked(pack[768:960, :]), right_form(misc[ROW_C : ROW_C + 128, :]))
@@ -698,8 +706,8 @@
             pltpu.VMEM((S0, CROSS + 512), F32),
             pltpu.VMEM((2, 128, 256), F32),
             pltpu.VMEM((2, 128, 128), F32),
-            pltpu.VMEM((768, 128), F32),
-            pltpu.VMEM((512, 128), F32),
+            pltpu.VMEM((256, 128), F32),
+            pltpu.VMEM((256, 128), F32),
             pltpu.VMEM((192, 128), F32),
             pltpu.VMEM((3, 128, 384), BF16),
             pltpu.VMEM((5, 384, 128), BF16),

time: 29.3 us -> 29 us (0.990)
  Pallas kernels: 27.6 us -> 27.3 us
    pallas_call x1, Pallas kernels: 25.5 us -> 25.1 us  [local(): pl.pallas_call(exchange, out_shape=(jax.ShapeDtypeStruct((S0, CROSS), F32...]
where the time goes in v3:
time: 29 us; the launch traced here: 28.6 us
  Pallas kernels  27.3 us (94%)
  between operations  1.32 us (5%)
    pallas_call x1, Pallas kernels, local(): pl.pallas_call(exchange, out_shape=(jax.ShapeDtypeStruct((S0, CROSS), F32...  25.1 us
    pallas_call x1, Pallas kernels, local(): pl.pallas_call(close, out_shape=(jax.ShapeDtypeStruct((1, S0, CROSS), F32...  2.11 us

profile of v3, /device:TPU:57, one launch (start us, length us, event | category | flops | bytes accessed | tf_op | source)
XLA Modules:
  0.0 28.6 jit_solution(11499949459725159319)
XLA Ops:
  1.3 0.0 copy-start
  1.3 0.0 copy-start.1
  1.3 25.1 %shard_map.95 = (f32[128,4096]{1,0:T(8,128)S(1)}, f32[960,128]{1,0:T(8,128)S(1)}) custom-call(s32[1]{0:T(128)S(6)} %copy.12.flags, s32[2,6]{1,0:T(2,128)} %faces_hbm.1, f32[1,128,4096]{2,1,0:T(8,128)} %now_hbm.1, f32[1,128,4096]{2,1,0:T(8,128)} %prev_hbm.1, f32[128,4096]{1,0:T(8,128)} %constant.8.clone.gain_hbm.gain, ...), custom_call_target="tpu_custom_call" | custom-call | tf_op jit(solution)/shard_map/pallas_call | solution.py:690
  26.5 0.0 copy-done
  26.5 0.0 copy-done.1
  26.5 2.1 %shard_map.96 = (f32[1,128,4096]{2,1,0:T(8,128)}, f32[192,128]{1,0:T(8,128)}) custom-call(s32[1]{0:T(128)S(6)} %copy.12.flags, f32[960,128]{1,0:T(8,128)S(1)} %get-tuple-element.6.pack, f32[1280,128]{1,0:T(8,128)S(1)} %copy-done.1, f32[128,4096]{1,0:T(8,128)S(1)} %get-tuple-element.7.free, f32[128,4096]{1,0:T(8,128)S(1)} %copy-done), custom_call_target="tpu_custom_call" | custom-call | tf_op jit(solution)/shard_map/pallas_call | solution.py:738
Async XLA Ops:
  1.3 25.2 %copy-start = (f32[128,4096]{1,0:T(8,128)S(1)}, f32[128,4096]{1,0:T(8,128)}, u32[]{:S(2)}) copy-start(f32[128,4096]{1,0:T(8,128)} %constant.8.clone.gain_hbm.gain) | copy-start | bytes 6291460
  1.3 25.2 %copy-start.1 = (f32[1280,128]{1,0:T(8,128)S(1)}, f32[1280,128]{1,0:T(8,128)}, u32[]{:S(2)}) copy-start(f32[1280,128]{1,0:T(8,128)} %constant.9.clone.misc_hbm.misc) | copy-start | bytes 1966084

commit v4 on v3

--- a/solution.py
+++ b/solution.py
@@ -13,6 +13,8 @@
 S2 = 64
 CROSS = S1 * S2
 STEPS = 3
+FORCES_AT = 1
+LAYERS_AT = (4, 5)
 TILES = CROSS // 128
 PLANE = 32
 MESH = pl.DeviceIdType.MESH
@@ -152,7 +154,7 @@
     flags, faces_hbm, now_hbm, prev_hbm, gain_hbm, misc_hbm, stencil_hbm, modes_hbm,
     free_out, pack_out,
     state, gain, slow, misc, modes, stencil, halved, rolled, tapped, rows,
-    acc, picked, free, left, right, flag_out, flag_in, layers, sums, low_in, force_in, pack,
+    acc, picked, free, left, right, flag_out, flag_in, layers, sums, low_in, force_in, pair_in, pack,
     faces, load_sem, send_sem, recv_sem, out_sem,
 ):
     gx, gy = lax.axis_index("gx"), lax.axis_index("gy")
@@ -181,6 +183,12 @@
     ]
     for load in rest:
         load.start()
+    core = lax.rem(gy, 2)
+    away = 2 * core - 1
+    other = -away
+    away_ok = jnp.where(core == 0, gy > 0, gy < ny - 1)
+    order = ((away, away_ok), (other, gy >= 0), (0, gy >= 0))
+
     back_ok, ahead_ok = gx > 0, gx < nx - 1
     side_ok = {-1: gy > 0, 0: gy >= 0, 1: gy < ny - 1}
     barrier = pltpu.get_barrier_semaphore()
@@ -191,61 +199,90 @@
             def _():
                 pl.semaphore_signal(barrier, inc=1, device_id=(to_x, gy + side), device_id_type=MESH)
 
+    pl.semaphore_signal(barrier, inc=1, device_id=(gx, gy + other), device_id_type=MESH)
     flag_out[...] = jnp.full(flag_out.shape, flags[0], jnp.int32).astype(F32)
 
-    core = lax.rem(gy, 2)
-    away = 2 * core - 1
-    away_ok = jnp.where(core == 0, gy > 0, gy < ny - 1)
-    order = ((away, away_ok), (-away, gy >= 0), (0, gy >= 0))
-
-    def back(source, target, sem, g):
+    def send(source, target, sem, to_x, to_y):
         return pltpu.make_async_remote_copy(
             src_ref=source, dst_ref=target, send_sem=send_sem.at[sem], recv_sem=recv_sem.at[sem],
-            device_id=(gx - 1, gy - g), device_id_type=MESH,
+            device_id=(to_x, to_y), device_id_type=MESH,
         )
 
-    def ahead(source, target, sem, g):
-        return pltpu.make_async_remote_copy(
-            src_ref=source, dst_ref=target, send_sem=send_sem.at[sem], recv_sem=recv_sem.at[sem],
-            device_id=(gx + 1, gy + g), device_id_type=MESH,
-        )
-
     def flag_copy(g):
-        return back(flag_out, flag_in.at[g + 1], g + 1, g)
-
-    def low_copy(n, g):
-        return back(layers.at[n, pl.ds(0, 96)], low_in.at[n, g + 1], 3 + 3 * n + g + 1, g)
-
-    def force_copy(n, g):
-        return ahead(sums.at[n, g + 1], force_in.at[n, g + 1], 12 + 3 * n + g + 1, g)
-
-    def send_back(copy):
-        for side, ok in order:
-
-            @pl.when(jnp.logical_and(back_ok, ok))
-            def _():
-                copy(-side).start()
-
-    def got_back(copy):
-        for g in (-1, 0, 1):
-
-            @pl.when(jnp.logical_and(ahead_ok, side_ok[g]))
-            def _():
-                copy(g).wait_recv()
-
-    def send_ahead(copy):
-        for side, ok in order:
-
-            @pl.when(jnp.logical_and(ahead_ok, ok))
-            def _():
-                copy(side).start()
-
-    def got_ahead(copy):
-        for g in (-1, 0, 1):
-
-            @pl.when(jnp.logical_and(back_ok, side_ok[-g]))
-            def _():
-                copy(g).wait_recv()
+        return send(flag_out, flag_in.at[g + 1], g + 1, gx - 1, gy - g)
+
+    half = (pl.ds(0, 48), pl.ds(48, 48))
+
+    def low_straight(n, h):
+        return send(layers.at[n, half[h]], low_in.at[n, 1, half[h]], 3 + 8 * n + h, gx - 1, gy)
+
+    def low_away(n):
+        return send(layers.at[n, pl.ds(0, 96)], low_in.at[n, 1 - away], 5 + 8 * n, gx - 1, gy + away)
+
+    def low_other(n):
+        return send(layers.at[n, half[0]], low_in.at[n, 1 - other, half[0]], 6 + 8 * n, gx - 1, gy + other)
+
+    def low_relay(n):
+        return send(low_in.at[n, 1, half[1]], low_in.at[n, 1 - other, half[1]], 7 + 8 * n, gx, gy + other)
+
+    def force_away(n):
+        return send(sums.at[n, away + 1], force_in.at[n, away + 1], 8 + 8 * n, gx + 1, gy + away)
+
+    def force_pair(n):
+        return send(sums.at[n, other + 1], pair_in.at[n], 9 + 8 * n, gx, gy + other)
+
+    def force_straight(n):
+        return send(sums.at[n, 3], force_in.at[n, 1], 10 + 8 * n, gx + 1, gy)
+
+    def send_back(n):
+        @pl.when(back_ok)
+        def _():
+            low_straight(n, 1).start()
+
+            @pl.when(away_ok)
+            def _():
+                low_away(n).start()
+
+            low_straight(n, 0).start()
+            low_other(n).start()
+
+    def send_ahead(n):
+        @pl.when(ahead_ok)
+        def _():
+            force_pair(n).start()
+
+            @pl.when(away_ok)
+            def _():
+                force_away(n).start()
+
+    def pass_forces(n):
+        force_pair(n).wait_recv()
+        sums[n, 3] = sums[n, 1] + pair_in[n]
+        force_straight(n).start()
+
+    def pass_layers(n):
+        low_straight(n, 1).wait_recv()
+        low_relay(n).start()
+
+    def got_back(n):
+        @pl.when(ahead_ok)
+        def _():
+            low_straight(n, 0).wait_recv()
+            low_other(n).wait_recv()
+            low_relay(n).wait_recv()
+
+            @pl.when(away_ok)
+            def _():
+                low_away(n).wait_recv()
+
+    def got_ahead(n):
+        @pl.when(back_ok)
+        def _():
+            force_straight(n).wait_recv()
+
+            @pl.when(away_ok)
+            def _():
+                force_away(n).wait_recv()
 
     def is_pml(shape):
         return jnp.full(shape, flags[0], jnp.int32) > 0
@@ -298,8 +335,13 @@
 
     sides = 1 + (gy > 0).astype(jnp.int32) + (gy < ny - 1).astype(jnp.int32)
     ends = (gx > 0).astype(jnp.int32) + (gx < nx - 1).astype(jnp.int32)
-    pl.semaphore_wait(barrier, sides * ends)
-    send_back(flag_copy)
+    pl.semaphore_wait(barrier, sides * ends + 1)
+    for side, ok in order:
+
+        @pl.when(jnp.logical_and(back_ok, ok))
+        def _():
+            flag_copy(-side).start()
+
 
     line = lax.broadcasted_iota(jnp.int32, (8, 128), 0)
 
@@ -350,7 +392,7 @@
 
     for e, plane in enumerate(gathered_faces()):
         layers[0, e * 32 : (e + 1) * 32, :] = plane
-    send_back(lambda g: low_copy(0, g))
+    send_back(0)
 
     def chosen(r, g):
         return jnp.logical_and(
@@ -379,10 +421,10 @@
         return couple([x + y for x, y in zip(a, b)])
 
     def low_force(n):
-        total = jnp.zeros((96, 128), F32)
-        for g in (-1, 0, 1):
-            there = jnp.logical_and(back_ok, side_ok[-g]).astype(jnp.int32)
-            total += jnp.where(jnp.full((96, 128), there, jnp.int32) > 0, force_in[n, g + 1], 0.0)
+        straight_there = jnp.full((96, 128), back_ok.astype(jnp.int32), jnp.int32) > 0
+        away_there = jnp.full((96, 128), jnp.logical_and(back_ok, away_ok).astype(jnp.int32), jnp.int32) > 0
+        total = jnp.where(straight_there, force_in[n, 1], 0.0)
+        total += jnp.where(away_there, force_in[n, 1 - away], 0.0)
         return total
 
     def response(force):
@@ -401,7 +443,7 @@
         return low + high
 
     make_sums(0)
-    send_ahead(lambda g: force_copy(0, g))
+    send_ahead(0)
     k = big_row.astype(F32)
     rate = 0.5 * ((k + 0.5) * (1.0 / S0)) ** 2
     inverse = 1.0 / (1.0 + rate)
@@ -468,6 +510,7 @@
                 turn[row, turn_here] = pltpu.roll(block, 64, 1)
 
     w1, w2 = TAPS_90[0], TAPS_90[1]
+    layers_at = jnp.where(lax.rem(gx, 4) == 3, LAYERS_AT[1], LAYERS_AT[0])
     small_first = lax.broadcasted_iota(jnp.int32, (32, 128), 1) < 64
 
     def keep_taps(cut, at, slot):
@@ -523,6 +566,15 @@
         @pl.loop(0, TILES // 4 - 1)
         def _(i):
             base = pl.multiple_of(i * 512, 512)
+
+            @pl.when(jnp.logical_and(ahead_ok, i == FORCES_AT))
+            def _():
+                pass_forces(n)
+
+            @pl.when(jnp.logical_and(ahead_ok, i == layers_at))
+            def _():
+                pass_layers(n)
+
             for s in range(2):
                 step(base, 4 * i + 2 * s, 256 * s, s, 2, 1024)
 
@@ -539,7 +591,12 @@
         return jnp.broadcast_to(value[0:1, :], (128, 128))
 
     def finish_matrices():
-        got_back(flag_copy)
+        for g in (-1, 0, 1):
+
+            @pl.when(jnp.logical_and(ahead_ok, side_ok[g]))
+            def _():
+                flag_copy(g).wait_recv()
+
         their = [theirs(r) for r in range(2)]
         their_col = jnp.where(big_col < 64, their[0], their[1]) > 0.5
         cross_one = jnp.where(their_col, one_pml, one_air)
@@ -558,18 +615,18 @@
     for n in range(STEPS):
         b, p = n % 2, 1 - n % 2
         if n > 0:
-            send_back(lambda g: low_copy(n, g))
+            send_back(n)
             make_sums(n)
-            send_ahead(lambda g: force_copy(n, g))
+            send_ahead(n)
             keep_force(force)
         advance(b, p, n)
         if n == 0:
             finish_matrices()
         if n == STEPS - 1:
             unforced.start()
-        got_back(lambda g: low_copy(n, g))
+        got_back(n)
         high = high_force(n)
-        got_ahead(lambda g: force_copy(n, g))
+        got_ahead(n)
         low = low_force(n)
         if n == 0:
             turned = dot(stacked(low), right[4])
@@ -591,13 +648,28 @@
         @pl.when(jnp.logical_and(back_ok, ok))
         def _():
             flag_copy(-side).wait_send()
-            for n in range(STEPS):
-                low_copy(n, -side).wait_send()
-
-        @pl.when(jnp.logical_and(ahead_ok, ok))
-        def _():
-            for n in range(STEPS):
-                force_copy(n, side).wait_send()
+
+    @pl.when(back_ok)
+    def _():
+        for n in range(STEPS):
+            low_straight(n, 0).wait_send()
+            low_straight(n, 1).wait_send()
+            low_other(n).wait_send()
+
+            @pl.when(away_ok)
+            def _():
+                low_away(n).wait_send()
+
+    @pl.when(ahead_ok)
+    def _():
+        for n in range(STEPS):
+            low_relay(n).wait_send()
+            force_pair(n).wait_send()
+            force_straight(n).wait_send()
+
+            @pl.when(away_ok)
+            def _():
+                force_away(n).wait_send()
 
     unforced.wait()
     packed.wait()
@@ -714,14 +786,15 @@
             pltpu.VMEM((8, 128), F32),
             pltpu.VMEM((3, 8, 128), F32),
             pltpu.VMEM((STEPS + 1, 192, 128), F32),
+            pltpu.VMEM((STEPS, 4, 96, 128), F32),
             pltpu.VMEM((STEPS, 3, 96, 128), F32),
             pltpu.VMEM((STEPS, 3, 96, 128), F32),
-            pltpu.VMEM((STEPS, 3, 96, 128), F32),
+            pltpu.VMEM((STEPS, 96, 128), F32),
             pltpu.VMEM((960, 128), F32),
             pltpu.SMEM((2, 6), jnp.int32),
             pltpu.SemaphoreType.DMA((10,)),
-            pltpu.SemaphoreType.DMA((21,)),
-            pltpu.SemaphoreType.DMA((21,)),
+            pltpu.SemaphoreType.DMA((27,)),
+            pltpu.SemaphoreType.DMA((27,)),
             pltpu.SemaphoreType.DMA((2,)),
         ],
         compiler_params=pltpu.CompilerParams(

time: 29 us -> 28.1 us (0.969)
  Pallas kernels: 27.3 us -> 26.6 us
    pallas_call x1, Pallas kernels: 25.1 us -> 24.5 us  [local(): pl.pallas_call(exchange, out_shape=(jax.ShapeDtypeStruct((S0, CROSS), F32...]
where the time goes in v4:
time: 28.1 us; the launch traced here: 28 us
  Pallas kernels  26.6 us (95%)
  between operations  1.32 us (5%)
    pallas_call x1, Pallas kernels, local(): pl.pallas_call(exchange, out_shape=(jax.ShapeDtypeStruct((S0, CROSS), F32...  24.5 us
    pallas_call x1, Pallas kernels, local(): pl.pallas_call(close, out_shape=(jax.ShapeDtypeStruct((1, S0, CROSS), F32...  2.11 us

profile of v4, /device:TPU:57, one launch (start us, length us, event | category | flops | bytes accessed | tf_op | source)
XLA Modules:
  0.0 28.0 jit_solution(286108083410189922)
XLA Ops:
  1.3 0.0 copy-start
  1.3 0.0 copy-start.1
  1.3 24.5 %shard_map.95 = (f32[128,4096]{1,0:T(8,128)S(1)}, f32[960,128]{1,0:T(8,128)S(1)}) custom-call(s32[1]{0:T(128)S(6)} %copy.12.flags, s32[2,6]{1,0:T(2,128)} %faces_hbm.1, f32[1,128,4096]{2,1,0:T(8,128)} %now_hbm.1, f32[1,128,4096]{2,1,0:T(8,128)} %prev_hbm.1, f32[128,4096]{1,0:T(8,128)} %constant.8.clone.gain_hbm.gain, ...), custom_call_target="tpu_custom_call" | custom-call | tf_op jit(solution)/shard_map/pallas_call | solution.py:762
  25.8 0.0 copy-done
  25.8 0.0 copy-done.1
  25.8 2.1 %shard_map.96 = (f32[1,128,4096]{2,1,0:T(8,128)}, f32[192,128]{1,0:T(8,128)}) custom-call(s32[1]{0:T(128)S(6)} %copy.12.flags, f32[960,128]{1,0:T(8,128)S(1)} %get-tuple-element.6.pack, f32[1280,128]{1,0:T(8,128)S(1)} %copy-done.1, f32[128,4096]{1,0:T(8,128)S(1)} %get-tuple-element.7.free, f32[128,4096]{1,0:T(8,128)S(1)} %copy-done), custom_call_target="tpu_custom_call" | custom-call | tf_op jit(solution)/shard_map/pallas_call | solution.py:811
Async XLA Ops:
  1.3 24.6 %copy-start = (f32[128,4096]{1,0:T(8,128)S(1)}, f32[128,4096]{1,0:T(8,128)}, u32[]{:S(2)}) copy-start(f32[128,4096]{1,0:T(8,128)} %constant.8.clone.gain_hbm.gain) | copy-start | bytes 6291460
  1.3 24.5 %copy-start.1 = (f32[1280,128]{1,0:T(8,128)S(1)}, f32[1280,128]{1,0:T(8,128)}, u32[]{:S(2)}) copy-start(f32[1280,128]{1,0:T(8,128)} %constant.9.clone.misc_hbm.misc) | copy-start | bytes 1966084

commit v5 on v4

--- a/solution.py
+++ b/solution.py
@@ -14,7 +14,7 @@
 CROSS = S1 * S2
 STEPS = 3
 FORCES_AT = 1
-LAYERS_AT = (4, 5)
+LAYERS_AT = (4, 6)
 TILES = CROSS // 128
 PLANE = 32
 MESH = pl.DeviceIdType.MESH
@@ -160,8 +160,14 @@
     gx, gy = lax.axis_index("gx"), lax.axis_index("gy")
     nx, ny = lax.axis_size("gx"), lax.axis_size("gy")
 
-    head = pltpu.make_async_copy(misc_hbm, misc, load_sem.at[0])
+    def table(first, last, sem):
+        at = pl.ds(first, last - first)
+        return pltpu.make_async_copy(misc_hbm.at[at], misc.at[at], load_sem.at[sem])
+
+    head = table(ROW_C, ROW_C + 512, 0)
     head.start()
+    weights_load = table(ROW_FACE, ROW_P, 10)
+    weights_load.start()
     listed = pltpu.make_async_copy(faces_hbm, faces, load_sem.at[8])
     listed.start()
     chunk = CROSS // 4
@@ -180,6 +186,7 @@
         pltpu.make_async_copy(prev_hbm.at[0], state.at[1, :, pl.ds(128, CROSS)], load_sem.at[2]),
         pltpu.make_async_copy(stencil_hbm, stencil, load_sem.at[3]),
         pltpu.make_async_copy(modes_hbm, modes, load_sem.at[9]),
+        table(ROW_P, ROW_C, 11),
     ]
     for load in rest:
         load.start()
@@ -376,6 +383,7 @@
             high.append(jnp.where(pml, row_high, even - odd))
         return low + high
 
+    weights_load.wait()
     for i in range(4):
         nows[i].wait()
 
@@ -458,22 +466,17 @@
     for c in (0, 1, TILES + 2, TILES + 3):
         rolled[:, c * 128 : (c + 1) * 128] = edge
     pack[192:768, :] = jnp.zeros((576, 128), F32)
+    rows[2] = center
+    rows[3] = mode_k
     rest[0].wait()
 
     def tile(c):
         return pl.ds(pl.multiple_of(c * 128, 128), 128)
-
-    @pl.loop(0, TILES)
-    def _(c):
-        col = c * 128 + lax.broadcasted_iota(jnp.int32, (1, 128), 1)
-        mode_a = (col >> 6).astype(F32) * (math.pi / S1)
-        mode_b = (col & 63).astype(F32) * (math.pi / S2)
-        wave = mode_k + (mode_a * mode_a + mode_b * mode_b)
-        slow[:, tile(c)] = jnp.where(own, center, 2.0 - gain[:, tile(c)] * wave)
 
     rest[1].wait()
     rest[2].wait()
     rest[3].wait()
+    rest[4].wait()
 
     def keep_force(force):
         pml = is_pml((PLANE, 128))
@@ -543,6 +546,13 @@
                     box_here = slice(at + 128 + h * 128, at + 256 + h * 128)
                     total = tapped[slot, row, h * 128 : (h + 1) * 128] + w2 * (line[h] + line[h + 2])
                     total += jnp.where(small_first, quads[h], quads[h + 1])
+                    if n == 0:
+                        col = (c0 + h) * 128 + lax.broadcasted_iota(jnp.int32, (1, 128), 1)
+                        mode_a = (col >> 6).astype(F32) * (math.pi / S1)
+                        mode_b = (col & 63).astype(F32) * (math.pi / S2)
+                        wave = rows[3, row, :] + (mode_a * mode_a + mode_b * mode_b)
+                        doubled = 2.0 - table[row, here] * wave
+                        own_slow[row, here] = jnp.where(is_pml((32, 128)), rows[2, row, :], doubled)
                     following = own_slow[row, here] * line[h + 1]
                     following -= rows[0, row, :] * old[row, box_here]
                     following += rows[1, row, :] * total
@@ -777,7 +787,7 @@
             pltpu.VMEM((256, CROSS), BF16),
             pltpu.VMEM((S0, CROSS + 512), F32),
             pltpu.VMEM((2, 128, 256), F32),
-            pltpu.VMEM((2, 128, 128), F32),
+            pltpu.VMEM((4, 128, 128), F32),
             pltpu.VMEM((256, 128), F32),
             pltpu.VMEM((256, 128), F32),
             pltpu.VMEM((192, 128), F32),
@@ -792,7 +802,7 @@
             pltpu.VMEM((STEPS, 96, 128), F32),
             pltpu.VMEM((960, 128), F32),
             pltpu.SMEM((2, 6), jnp.int32),
-            pltpu.SemaphoreType.DMA((10,)),
+            pltpu.SemaphoreType.DMA((12,)),
             pltpu.SemaphoreType.DMA((27,)),
             pltpu.SemaphoreType.DMA((27,)),
             pltpu.SemaphoreType.DMA((2,)),

time: 28.1 us -> 28 us (level)
  no operation moved by 1% of the time
where the time goes in v5:
time: 28 us; the launch traced here: 27.9 us
  Pallas kernels  26.5 us (95%)
  between operations  1.32 us (5%)
    pallas_call x1, Pallas kernels, local(): pl.pallas_call(exchange, out_shape=(jax.ShapeDtypeStruct((S0, CROSS), F32...  24.5 us
    pallas_call x1, Pallas kernels, local(): pl.pallas_call(close, out_shape=(jax.ShapeDtypeStruct((1, S0, CROSS), F32...  2.06 us

profile of v5, /device:TPU:57, one launch (start us, length us, event | category | flops | bytes accessed | tf_op | source)
XLA Modules:
  0.0 27.9 jit_solution(12773245802432156794)
XLA Ops:
  1.3 0.0 copy-start
  1.3 0.0 copy-start.1
  1.3 24.5 %shard_map.95 = (f32[128,4096]{1,0:T(8,128)S(1)}, f32[960,128]{1,0:T(8,128)S(1)}) custom-call(s32[1]{0:T(128)S(6)} %copy.12.flags, s32[2,6]{1,0:T(2,128)} %faces_hbm.1, f32[1,128,4096]{2,1,0:T(8,128)} %now_hbm.1, f32[1,128,4096]{2,1,0:T(8,128)} %prev_hbm.1, f32[128,4096]{1,0:T(8,128)} %constant.8.clone.gain_hbm.gain, ...), custom_call_target="tpu_custom_call" | custom-call | tf_op jit(solution)/shard_map/pallas_call | solution.py:772
  25.8 0.0 copy-done
  25.8 0.0 copy-done.1
  25.8 2.1 %shard_map.96 = (f32[1,128,4096]{2,1,0:T(8,128)}, f32[192,128]{1,0:T(8,128)}) custom-call(s32[1]{0:T(128)S(6)} %copy.12.flags, f32[960,128]{1,0:T(8,128)S(1)} %get-tuple-element.6.pack, f32[1280,128]{1,0:T(8,128)S(1)} %copy-done.1, f32[128,4096]{1,0:T(8,128)S(1)} %get-tuple-element.7.free, f32[128,4096]{1,0:T(8,128)S(1)} %copy-done), custom_call_target="tpu_custom_call" | custom-call | tf_op jit(solution)/shard_map/pallas_call | solution.py:821
Async XLA Ops:
  1.3 24.5 %copy-start = (f32[128,4096]{1,0:T(8,128)S(1)}, f32[128,4096]{1,0:T(8,128)}, u32[]{:S(2)}) copy-start(f32[128,4096]{1,0:T(8,128)} %constant.8.clone.gain_hbm.gain) | copy-start | bytes 6291460
  1.3 24.5 %copy-start.1 = (f32[1280,128]{1,0:T(8,128)S(1)}, f32[1280,128]{1,0:T(8,128)}, u32[]{:S(2)}) copy-start(f32[1280,128]{1,0:T(8,128)} %constant.9.clone.misc_hbm.misc) | copy-start | bytes 1966084
